TPU v7x, 128 devices: a whole 4x4x4 slice. The times are simulated.
128 devices in a mesh: ctx: 16 (over z, x_lo, core), tp: 8 (over y, x_hi).
Axes of the slice: x: 4 (x_hi: 2, x_lo: 2; x = x_hi * 2 + x_lo), y: 4, z: 4, core: 2. Of those that a mesh axis runs over, the one named last changes fastest.
Arguments:
- projected: bfloat16 [3, 4096, 8192], P(None, 'ctx', 'tp'), may hold values from -6 to 6
- short_taps: float32 [3, 7, 8192], P(None, None, 'tp'), may hold values from -2.4 to 2.4
- range_filter: bfloat16 [64, 1024], P('tp'), may hold values from -0.1875 to 0.1875
- skip_gain: float32 [8192], P('tp'), may hold values from -4 to 4
- out_weight: bfloat16 [8192, 8192], P('ctx', 'tp'), may hold values from -0.0625 to 0.0625
Outputs:
- mixed: bfloat16 [4096, 8192], P('ctx', 'tp')
All inputs are finite; a program needn't handle non-finite values.
Results may differ from a plain program's by a relative error of at most 0.0057.
Values may be sent and summed in bfloat16 or wider, within the bound.
A program may use at most 192 MiB of HBM per device.

v0:
```python
import jax
import jax.numpy as jnp
from jax import lax
from jax.sharding import PartitionSpec as P


def passed_along(block, axis, distance):
    devices = range(lax.axis_size(axis))
    route = [((i - distance) % len(devices), i) for i in devices]
    return lax.ppermute(block, axis, route)


def short_conv(extended, tap_rows, length):
    accumulated = jnp.zeros((length, extended.shape[1]), jnp.float32)
    rim_width = tap_rows.shape[0] - 1
    for lag_index in range(tap_rows.shape[0]):
        window = extended[rim_width - lag_index : rim_width - lag_index + length]
        accumulated = accumulated + tap_rows[lag_index][None, :] * window.astype(jnp.float32)
    return accumulated


def toeplitz_slabs(range_filter, length, span_blocks):
    kept = range_filter.shape[1]
    offsets = lax.broadcasted_iota(jnp.int32, (span_blocks + 1, length, length), 0)
    rows_at = lax.broadcasted_iota(jnp.int32, (span_blocks + 1, length, length), 1)
    cols_at = lax.broadcasted_iota(jnp.int32, (span_blocks + 1, length, length), 2)
    lag_at = offsets * length + rows_at - cols_at
    inside = jnp.logical_and(lag_at >= 0, lag_at < kept)
    clipped = jnp.clip(lag_at, 0, kept - 1)
    looked = jnp.take(range_filter, clipped.reshape(-1), axis=1).reshape(
        range_filter.shape[0], span_blocks + 1, length, length
    )
    return jnp.where(inside[None], looked, jnp.zeros((), range_filter.dtype))


def local(projected, short_taps, range_filter, skip_gain, out_weight):
    length = projected.shape[1]
    width_dev = projected.shape[2]
    groups = range_filter.shape[0]
    group_width = width_dev // groups
    rim_width = short_taps.shape[1] - 1
    span_blocks = range_filter.shape[1] // length
    rim_block = passed_along(projected[:, length - rim_width :, :], "ctx", 1)
    extended = jnp.concatenate([rim_block, projected], axis=1)
    query_feat = short_conv(extended[0], short_taps[0], length)
    key_feat = short_conv(extended[1], short_taps[1], length)
    value_feat = short_conv(extended[2], short_taps[2], length)
    mixed_in = (key_feat * value_feat).astype(jnp.bfloat16)
    slabs = toeplitz_slabs(range_filter, length, span_blocks)

    def correlate(arrived, offset):
        grouped = arrived.reshape(length, groups, group_width)
        product = jnp.einsum(
            "gam,mgc->agc", slabs[:, offset], grouped, preferred_element_type=jnp.float32
        )
        return product.reshape(length, width_dev)

    toeplitz = correlate(mixed_in, 0)
    for offset in range(1, span_blocks + 1):
        arrived = passed_along(mixed_in, "ctx", offset)
        toeplitz = toeplitz + correlate(arrived, offset)
    restored = lax.optimization_barrier(mixed_in).astype(jnp.float32)
    gated_out = (query_feat * (toeplitz + skip_gain[None, :] * restored)).astype(jnp.bfloat16)
    gathered = lax.all_gather(gated_out, "tp", axis=1, tiled=True)
    summed = jnp.dot(
        gathered,
        lax.all_gather(out_weight, "ctx", axis=0, tiled=True),
        preferred_element_type=jnp.float32,
    )
    return summed.astype(jnp.bfloat16)


def solution(mesh):
    placed = (P(None, "ctx", "tp"), P(None, None, "tp"), P("tp", None), P("tp"), P("ctx", "tp"))
    return jax.shard_map(
        local, mesh=mesh, in_specs=placed, out_specs=P("ctx", "tp"), check_vma=False
    )
```

profile of v0, /device:TPU:1, one launch (start us, length us, event | category | flops | bytes accessed | tf_op | source)
XLA Modules:
  0.0 1476.2 jit_solution(5024653289956213897)
XLA Ops:
  8.0 2.6 collective-permute-start
  15.7 1133.3 %gather_fusion = bf16[327680,8]{1,0:T(8,128)(2,1)} fusion(bf16[8,1024]{0,1:T(8,128)(2,1)S(1)} %copy.40, s32[327680]{0:T(1024)S(1)} %broadcast_clamp_fusion), kind=kCustom, calls=%fused_computation | custom fusion | bytes 11796480 | tf_op jit(solution)/shard_map/jit(_take)/gather | solution.py:30
  1149.1 60.1 %copy.42 = bf16[8,5,256,256]{3,2,0,1:T(8,128)(2,1)} copy(bf16[8,5,256,256]{0,3,2,1:T(8,128)(2,1)} %bitcast.44) | data formatting | bytes 10485760 | tf_op jit(solution)/shard_map/jit(_take)/gather | solution.py:30
  1209.2 6.1 select_select_fusion
  1216.3 3.8 fusion.19
  1227.5 3.4 fusion.58
  1230.9 2.5 copy.60
  1233.5 2.5 copy.59
  1238.6 2.6 copy.57
  1242.4 3.9 fusion.46
  1246.4 2.6 copy.55
  1249.0 2.5 copy.54
  1256.6 2.6 copy.51
  1259.2 2.5 copy.50
  1263.0 2.6 copy.48
  1265.7 7.1 fusion.8
  1275.1 2.9 fusion.6
  1280.0 2.7 fusion.7
  1282.7 2.7 convolution_add_fusion.1
  1286.8 3.3 fusion.1
  1291.8 3.0 fusion.11
  1295.6 69.1 %all-gather.3.cloned.1.call-done = bf16[256,8192]{1,0:T(8,128)(2,1)} async-done(((bf16[256,1024]{1,0:T(8,128)(2,1)}), bf16[256,8192]{1,0:T(8,128)(2,1)}) %all-gather.3.cloned.1.call-update) | async-done | bytes 4194320 | tf_op jit(solution)/shard_map/all_gather | solution.py:64
  1364.7 92.4 %all-gather.5.cloned.1.call-done = bf16[8192,1024]{1,0:T(8,128)(2,1)} async-done(((bf16[512,1024]{1,0:T(8,128)(2,1)}), bf16[8192,1024]{1,0:T(8,128)(2,1)}) %all-gather.5.cloned.1.call-update) | async-done | bytes 16777232 | tf_op jit(solution)/shard_map/all_gather | solution.py:67
  1457.1 12.3 convolution_convert_fusion
  (92 shorter events, 33.2 us)
Async XLA Ops:
  6.5 5.4 copy-start.3
  6.5 6.1 copy-start.20
  6.5 1358.2 %all-gather.3.cloned.1.call-start = ((), (), s32[]{:S(2)}) async-start(), calls=%async_computation | async-start | bytes 4718592 | tf_op jit(solution)/shard_map/all_gather | solution.py:64
  8.0 1208.2 %collective-permute-start = (bf16[3,6,1024]{2,1,0:T(8,128)(2,1)}, bf16[3,6,1024]{2,1,0:T(8,128)(2,1)}, u32[]{:S(2)}, u32[]{:S(2)}) collective-permute-start(bf16[3,6,1024]{2,1,0:T(8,128)(2,1)} %slice.240), channel_id=1, source_target_pairs={{120,0},{0,8},{8,16},{16,24},{24,32},{32,40},{40,48},{48,56},{56,6... | collective-permute-start | bytes 110600 | tf_op jit(solution)/shard_map/ppermute | solution.py:10
  1209.1 7.1 copy-start
  1209.2 7.1 copy-start.4
  1209.2 7.1 copy-start.6
  1209.2 7.1 copy-start.8
  1209.2 7.1 copy-start.10
  1209.2 7.1 copy-start.12
  1209.2 7.1 copy-start.14
  1209.2 7.1 copy-start.16
  1209.2 7.1 copy-start.18
  1220.1 52.7 %collective-permute-start.4 = (bf16[256,1024]{1,0:T(8,128)(2,1)}, bf16[256,1024]{1,0:T(8,128)(2,1)S(1)}, u32[]{:S(2)}, u32[]{:S(2)}) collective-permute-start(bf16[256,1024]{1,0:T(8,128)(2,1)} %get-tuple-element.5), channel_id=1, source_target_pairs={{96,0},{104,8},{112,16},{120,24},{0,32},{8,40},{16,48},{24,56},{32... | collective-permute-start | bytes 1572872 | tf_op jit(solution)/shard_map/ppermute | solution.py:10
  1221.8 52.0 %collective-permute-start.3 = (bf16[256,1024]{1,0:T(8,128)(2,1)}, bf16[256,1024]{1,0:T(8,128)(2,1)}, u32[]{:S(2)}, u32[]{:S(2)}) collective-permute-start(bf16[256,1024]{1,0:T(8,128)(2,1)} %get-tuple-element.5), channel_id=1, source_target_pairs={{104,0},{112,8},{120,16},{0,24},{8,32},{16,40},{24,48},{32,56},{40... | collective-permute-start | bytes 1572872 | tf_op jit(solution)/shard_map/ppermute | solution.py:10
  1222.5 55.4 %collective-permute-start.1 = (bf16[256,1024]{1,0:T(8,128)(2,1)}, bf16[256,1024]{1,0:T(8,128)(2,1)}, u32[]{:S(2)}, u32[]{:S(2)}) collective-permute-start(bf16[256,1024]{1,0:T(8,128)(2,1)} %get-tuple-element.5), channel_id=1, source_target_pairs={{120,0},{0,8},{8,16},{16,24},{24,32},{32,40},{40,48},{48,56},{56,6... | collective-permute-start | bytes 1572872 | tf_op jit(solution)/shard_map/ppermute | solution.py:10
  1224.9 60.5 %collective-permute-start.2 = (bf16[256,1024]{1,0:T(8,128)(2,1)}, bf16[256,1024]{1,0:T(8,128)(2,1)}, u32[]{:S(2)}, u32[]{:S(2)}) collective-permute-start(bf16[256,1024]{1,0:T(8,128)(2,1)} %get-tuple-element.5), channel_id=1, source_target_pairs={{112,0},{120,8},{0,16},{8,24},{16,32},{24,40},{32,48},{40,56},{48,... | collective-permute-start | bytes 1572872 | tf_op jit(solution)/shard_map/ppermute | solution.py:10
  1261.7 3.9 copy-start.9
  1261.7 3.9 copy-start.11
  1261.7 3.9 copy-start.13
  1261.7 3.9 copy-start.15
  1261.7 3.9 copy-start.17
  1261.7 3.9 copy-start.19
  1294.8 162.2 %all-gather.5.cloned.1.call-start = ((), (), s32[]{:S(2)}) async-start(), calls=%async_computation.1 | async-start | bytes 17825792 | tf_op jit(solution)/shard_map/all_gather | solution.py:67
  (12 other events, 25.1 us)
Sparse Core Ops, SparseCore 0:
  1295.0 69.6 all-gather.2
  1366.4 90.6 all-gather.4
where the time goes:
time: 1480 us
  local copies, waits for them, and re-layouts  1240 us (84%)
  waiting for transfers between devices  162 us (11%)
  matrix products  31.1 us (2%)
  other arithmetic  23.1 us (2%)
    gather x2, local copies, waits for them, and re-layouts, toeplitz_slabs(): jnp.take(range_filter, clipped.reshape(-1), axis=1)  1190 us
    all_gather x1, waiting for transfers between devices, local(): lax.all_gather(out_weight, 'ctx', axis=0, tiled=True)  92.4 us
    all_gather x1, waiting for transfers between devices, local(): gathered = lax.all_gather(gated_out, 'tp', axis=1, tiled=True)  69.1 us
    convert_element_type x14, local copies, waits for them, and re-layouts, short_conv(): window.astype(jnp.float32)  32 us
  transfers between devices with their start and end apart: 7, of which 2 were waited for; matrix products, arithmetic and copies ran while one was open for 86% of the time, Pallas kernels for 0%

commit v1 on v0

--- a/solution.py
+++ b/solution.py
@@ -19,18 +19,15 @@
     return accumulated
 
 
-def toeplitz_slabs(range_filter, length, span_blocks):
-    kept = range_filter.shape[1]
-    offsets = lax.broadcasted_iota(jnp.int32, (span_blocks + 1, length, length), 0)
-    rows_at = lax.broadcasted_iota(jnp.int32, (span_blocks + 1, length, length), 1)
-    cols_at = lax.broadcasted_iota(jnp.int32, (span_blocks + 1, length, length), 2)
-    lag_at = offsets * length + rows_at - cols_at
-    inside = jnp.logical_and(lag_at >= 0, lag_at < kept)
-    clipped = jnp.clip(lag_at, 0, kept - 1)
-    looked = jnp.take(range_filter, clipped.reshape(-1), axis=1).reshape(
-        range_filter.shape[0], span_blocks + 1, length, length
-    )
-    return jnp.where(inside[None], looked, jnp.zeros((), range_filter.dtype))
+def toeplitz_strip(range_filter, length):
+    groups, kept = range_filter.shape
+    period = kept + 2 * length
+    flipped = range_filter[:, ::-1]
+    row = jnp.pad(flipped, ((0, 0), (length, period - length - kept)))
+    tiled = jnp.tile(row, (1, length + 1))
+    start = length - 1
+    shifted = tiled[:, start : start + length * (period - 1)].reshape(groups, length, period - 1)
+    return shifted[:, :, : kept + length]
 
 
 def local(projected, short_taps, range_filter, skip_gain, out_weight):
@@ -46,19 +43,11 @@
     key_feat = short_conv(extended[1], short_taps[1], length)
     value_feat = short_conv(extended[2], short_taps[2], length)
     mixed_in = (key_feat * value_feat).astype(jnp.bfloat16)
-    slabs = toeplitz_slabs(range_filter, length, span_blocks)
-
-    def correlate(arrived, offset):
-        grouped = arrived.reshape(length, groups, group_width)
-        product = jnp.einsum(
-            "gam,mgc->agc", slabs[:, offset], grouped, preferred_element_type=jnp.float32
-        )
-        return product.reshape(length, width_dev)
-
-    toeplitz = correlate(mixed_in, 0)
-    for offset in range(1, span_blocks + 1):
-        arrived = passed_along(mixed_in, "ctx", offset)
-        toeplitz = toeplitz + correlate(arrived, offset)
+    strip = toeplitz_strip(range_filter, length)
+    pieces = [passed_along(mixed_in, "ctx", offset) for offset in range(span_blocks, 0, -1)]
+    window = jnp.concatenate(pieces + [mixed_in], axis=0).reshape(-1, groups, group_width)
+    toeplitz = jnp.einsum("gam,mgc->agc", strip, window, preferred_element_type=jnp.float32)
+    toeplitz = toeplitz.reshape(length, width_dev)
     restored = lax.optimization_barrier(mixed_in).astype(jnp.float32)
     gated_out = (query_feat * (toeplitz + skip_gain[None, :] * restored)).astype(jnp.bfloat16)
     gathered = lax.all_gather(gated_out, "tp", axis=1, tiled=True)

time: 1480 us -> 259 us (0.17)
  local copies, waits for them, and re-layouts: 1240 us -> 45.5 us
  other arithmetic: 23.1 us -> 7.04 us
    gather x2 -> x0, local copies, waits for them, and re-layouts: 1190 us -> none  [toeplitz_slabs(): jnp.take(range_filter, clipped.reshape(-1), axis=1)]
    convert_element_type x14 -> x0, local copies, waits for them, and re-layouts: 32 us -> none  [short_conv(): window.astype(jnp.float32)]
    unnamed x59 -> x11, local copies, waits for them, and re-layouts: 0.32 us -> 18.2 us
    reshape x0 -> x2, local copies, waits for them, and re-layouts: none -> 15.4 us  [the longest x1 13.7 us: toeplitz_strip(): tiled[:, start:start + length * (period - 1)]]
  transfers between devices with their start and end apart: 7 -> 7, of which waited for: 2 -> 3; matrix products, arithmetic and copies ran while one was open for 86% -> 15% of each run, Pallas kernels for 0% -> 0%
where the time goes in v1:
time: 259 us
  waiting for transfers between devices  166 us (64%)
  local copies, waits for them, and re-layouts  45.5 us (18%)
  matrix products  17.6 us (7%)
  between operations  13.5 us (5%)
  starting transfers between devices  9.11 us (4%)
  other arithmetic  7.04 us (3%)
    all_gather x1, waiting for transfers between devices, local(): lax.all_gather(out_weight, 'ctx', axis=0, tiled=True)  92.4 us
    all_gather x1, waiting for transfers between devices, local(): gathered = lax.all_gather(gated_out, 'tp', axis=1, tiled=True)  72 us
    unnamed x11, local copies, waits for them, and re-layouts  18.2 us
    reshape x1, local copies, waits for them, and re-layouts, toeplitz_strip(): tiled[:, start:start + length * (period - 1)]  13.7 us
    dot_general x1, matrix products, local(): jnp.dot(gathered, lax.all_gather(out_weight, 'ctx', axis=0, tiled=True),...  12.3 us
    ppermute x5, starting transfers between devices, passed_along(): return lax.ppermute(block, axis, route)  9.06 us
    dot_general x1, matrix products, local(): jnp.einsum('gam,mgc->agc', strip, window, preferred_element_type=jnp.floa...  5.29 us
    convert_element_type x1, other arithmetic, local(): mixed_in = (key_feat * value_feat).astype(jnp.bfloat16)  5.2 us
  transfers between devices with their start and end apart: 7, of which 3 were waited for; matrix products, arithmetic and copies ran while one was open for 15% of the time, Pallas kernels for 0%

profile of v1, /device:TPU:1, one launch (start us, length us, event | category | flops | bytes accessed | tf_op | source)
XLA Modules:
  0.0 258.7 jit_solution(12750595578099567330)
XLA Ops:
  6.5 0.8 slice.231
  7.4 2.7 %collective-permute-start = (bf16[3,6,1024]{2,1,0:T(8,128)(2,1)S(1)}, bf16[3,6,1024]{2,1,0:T(8,128)(2,1)S(1)}, u32[]{:S(2)}, u32[]{:S(2)}) collective-permute-start(bf16[3,6,1024]{2,1,0:T(8,128)(2,1)S(1)} %slice.231), channel_id=1, source_target_pairs={{120,0},{0,8},{8,16},{16,24},{24,32},{32,40},{40,48},{48,56},{56,6... | collective-permute-start | bytes 110600 | tf_op jit(solution)/shard_map/ppermute | solution.py:10
  10.0 1.4 fusion.59
  11.5 0.8 fusion.60
  12.3 5.2 %fusion.4 = bf16[256,1024]{1,0:T(8,128)(2,1)S(1)} fusion(bf16[3,6,1024]{2,1,0:T(8,128)(2,1)S(1)} %collective-permute-done, bf16[3,256,1024]{2,1,0:T(8,128)(2,1)} %param.5, f32[1024]{0:T(1024)S(1)} %bitcast.144, f32[1024]{0:T(1024)S(1)} %bitcast.143, f32[1024]{0:T(1024)S(1)} %bitcast.131, f32[1024]{0:T(1024)S(1)} %bitcast.132, f32[1024]{0:T(1024)S(1)} %bitcast.133, ...), kind=kLoop, calls=%fused_computation.23 | loop fusion | flops 23592960 | bytes 3239936 | tf_op jit(solution)/shard_map/convert_element_type | solution.py:45
  17.5 1.7 collective-permute-start.1
  19.2 2.8 %collective-permute-start.2 = (bf16[256,1024]{1,0:T(8,128)(2,1)S(1)}, bf16[256,1024]{1,0:T(8,128)(2,1)S(1)}, u32[]{:S(2)}, u32[]{:S(2)}) collective-permute-start(bf16[256,1024]{1,0:T(8,128)(2,1)S(1)} %fusion.4), channel_id=1, source_target_pairs={{104,0},{112,8},{120,16},{0,24},{8,32},{16,40},{24,48},{32,56},{40... | collective-permute-start | bytes 1572872 | tf_op jit(solution)/shard_map/ppermute | solution.py:10
  22.3 1.6 collective-permute-start.4
  25.0 3.9 %slice.307 = bf16[8,392960]{1,0:T(8,128)(2,1)} slice(bf16[8,394752]{1,0:T(8,128)(2,1)S(1)} %bitcast.128), slice={[0:8], [255:393215]} | slice | bytes 12574720 | tf_op jit(solution)/shard_map/slice | solution.py:29
  28.9 14.7 %reshape.143 = bf16[3143680]{0:T(1024)(128)(2,1)} reshape(bf16[8,392960]{1,0:T(8,128)(2,1)} %slice.307) | data formatting | bytes 12574720
  43.6 13.7 %reshape.120 = bf16[8,256,1535]{2,1,0:T(8,128)(2,1)} reshape(bf16[3143680]{0:T(1024)(128)(2,1)} %reshape.143) | data formatting | bytes 12574720 | tf_op jit(solution)/shard_map/reshape | solution.py:29
  57.4 0.8 constant_dynamic-update-slice_fusion.4
  58.2 0.9 collective-permute-done.2
  59.1 0.8 constant_dynamic-update-slice_fusion.3
  59.9 0.8 constant_dynamic-update-slice_fusion.2
  60.7 0.9 constant_dynamic-update-slice_fusion.1
  61.6 0.9 constant_dynamic-update-slice_fusion
  62.5 3.0 %copy.8 = bf16[1280,1024]{0,1:T(8,128)(2,1)S(1)} copy(bf16[1280,1024]{1,0:T(8,128)(2,1)} %constant_dynamic-update-slice_fusion) | data formatting | bytes 5242880 | tf_op jit(solution)/shard_map/concatenate | solution.py:48
  65.5 5.3 %fusion = f32[8,128,256]{2,1,0:T(8,128)} fusion(bf16[1280,8,128]{0,2,1:T(8,128)(2,1)S(1)} %bitcast.129, bf16[8,256,1535]{2,1,0:T(8,128)(2,1)} %reshape.120), kind=kOutput, calls=%fused_computation.17 | convolution fusion | flops 671088640 | bytes 8912896 | tf_op jit(solution)/shard_map/gam,mgc->agc/dot_general | solution.py:49
  70.8 1.7 copy.9
  72.5 1.8 fusion.18
  75.1 72.0 %all-gather.3.cloned.1.call-done = bf16[256,8192]{1,0:T(8,128)(2,1)} async-done(((bf16[256,1024]{1,0:T(8,128)(2,1)}), bf16[256,8192]{1,0:T(8,128)(2,1)}) %all-gather.3.cloned.1.call-update) | async-done | bytes 4194320 | tf_op jit(solution)/shard_map/all_gather | solution.py:53
  147.1 92.4 %all-gather.5.cloned.1.call-done = bf16[8192,1024]{1,0:T(8,128)(2,1)} async-done(((bf16[512,1024]{1,0:T(8,128)(2,1)}), bf16[8192,1024]{1,0:T(8,128)(2,1)}) %all-gather.5.cloned.1.call-update) | async-done | bytes 16777232 | tf_op jit(solution)/shard_map/all_gather | solution.py:56
  239.5 12.3 %convolution_convert_fusion = bf16[256,1024]{1,0:T(8,128)(2,1)} fusion(bf16[256,8192]{1,0:T(8,128)(2,1)} %all-gather.3.cloned.1.call-done, bf16[8192,1024]{1,0:T(8,128)(2,1)} %all-gather.5.cloned.1.call-done), kind=kOutput, calls=%fused_computation.19 | convolution fusion | flops 4295229440 | bytes 21495808 | tf_op jit(solution)/shard_map/dot_general | solution.py:54
  (18 shorter events, 2.2 us)
Async XLA Ops:
  6.5 17.4 %copy-start.1 = (bf16[8,1024]{1,0:T(8,128)(2,1)S(1)}, bf16[8,1024]{1,0:T(8,128)(2,1)}, u32[]{:S(2)}) copy-start(bf16[8,1024]{1,0:T(8,128)(2,1)} %param.7) | copy-start | bytes 49156
  6.5 140.6 %all-gather.3.cloned.1.call-start = ((), (), s32[]{:S(2)}) async-start(), calls=%async_computation | async-start | bytes 4718592 | tf_op jit(solution)/shard_map/all_gather | solution.py:53
  7.4 4.9 %collective-permute-start = (bf16[3,6,1024]{2,1,0:T(8,128)(2,1)S(1)}, bf16[3,6,1024]{2,1,0:T(8,128)(2,1)S(1)}, u32[]{:S(2)}, u32[]{:S(2)}) collective-permute-start(bf16[3,6,1024]{2,1,0:T(8,128)(2,1)S(1)} %slice.231), channel_id=1, source_target_pairs={{120,0},{0,8},{8,16},{16,24},{24,32},{32,40},{40,48},{48,56},{56,6... | collective-permute-start | bytes 110600 | tf_op jit(solution)/shard_map/ppermute | solution.py:10
  17.5 39.8 %collective-permute-start.1 = (bf16[256,1024]{1,0:T(8,128)(2,1)S(1)}, bf16[256,1024]{1,0:T(8,128)(2,1)S(1)}, u32[]{:S(2)}, u32[]{:S(2)}) collective-permute-start(bf16[256,1024]{1,0:T(8,128)(2,1)S(1)} %fusion.4), channel_id=1, source_target_pairs={{96,0},{104,8},{112,16},{120,24},{0,32},{8,40},{16,48},{24,56},{32... | collective-permute-start | bytes 1572872 | tf_op jit(solution)/shard_map/ppermute | solution.py:10
  19.2 39.8 %collective-permute-start.2 = (bf16[256,1024]{1,0:T(8,128)(2,1)S(1)}, bf16[256,1024]{1,0:T(8,128)(2,1)S(1)}, u32[]{:S(2)}, u32[]{:S(2)}) collective-permute-start(bf16[256,1024]{1,0:T(8,128)(2,1)S(1)} %fusion.4), channel_id=1, source_target_pairs={{104,0},{112,8},{120,16},{0,24},{8,32},{16,40},{24,48},{32,56},{40... | collective-permute-start | bytes 1572872 | tf_op jit(solution)/shard_map/ppermute | solution.py:10
  22.0 37.8 %collective-permute-start.3 = (bf16[256,1024]{1,0:T(8,128)(2,1)S(1)}, bf16[256,1024]{1,0:T(8,128)(2,1)S(1)}, u32[]{:S(2)}, u32[]{:S(2)}) collective-permute-start(bf16[256,1024]{1,0:T(8,128)(2,1)S(1)} %fusion.4), channel_id=1, source_target_pairs={{112,0},{120,8},{0,16},{8,24},{16,32},{24,40},{32,48},{40,56},{48,... | collective-permute-start | bytes 1572872 | tf_op jit(solution)/shard_map/ppermute | solution.py:10
  22.3 38.4 %collective-permute-start.4 = (bf16[256,1024]{1,0:T(8,128)(2,1)S(1)}, bf16[256,1024]{1,0:T(8,128)(2,1)S(1)}, u32[]{:S(2)}, u32[]{:S(2)}) collective-permute-start(bf16[256,1024]{1,0:T(8,128)(2,1)S(1)} %fusion.4), channel_id=1, source_target_pairs={{120,0},{0,8},{8,16},{16,24},{24,32},{32,40},{40,48},{48,56},{56,6... | collective-permute-start | bytes 1572872 | tf_op jit(solution)/shard_map/ppermute | solution.py:10
  65.4 7.0 %copy-start.2 = (f32[1024]{0:T(1024)S(1)}, f32[1024]{0:T(1024)}, u32[]{:S(2)}) copy-start(f32[1024]{0:T(1024)} %param.8) | copy-start | bytes 12292
  70.8 1.7 copy-start
  74.3 165.1 %all-gather.5.cloned.1.call-start = ((), (), s32[]{:S(2)}) async-start(), calls=%async_computation.1 | async-start | bytes 17825792 | tf_op jit(solution)/shard_map/all_gather | solution.py:56
Sparse Core Ops, SparseCore 0:
  74.5 72.6 all-gather.2
  148.8 90.6 all-gather.4

commit v2 on v1

v2 whole, which is shorter than its diff:
```python
import functools

import jax
import jax.numpy as jnp
from jax import lax
from jax.experimental import pallas as pl
from jax.experimental.pallas import tpu as pltpu
from jax.sharding import PartitionSpec as P

MESH = pl.DeviceIdType.MESH
RIM = 16
CHUNKS = 4
RING = 4
QUAD = 4
UPWARD = (2,)
ORDER = (3, 2, 1, 0)


def short_conv(extended, tap_rows):
    acc = tap_rows[0] * extended[RIM:]
    for lag in range(1, len(tap_rows)):
        acc = acc + tap_rows[lag] * pltpu.roll(extended, lag, axis=0)[RIM:]
    return acc


def kernel(
    proj, taps, filt, gain, w, out,
    rim, qext, qfeat, mixsend, seq, flipped, strip, abuf, wbuf, csend, crecv,
    rim_s, rim_r, q_s, q_r, qrim_s, qrim_r, mix_s, mix_r, halo_s, halo_r,
    wx_s, wx_r, wz_s, wz_r, w2_s, w2_r, a_s, a_r, a2_s, a2_r, p_s, p_r, c_s, c_r,
):
    length = proj.shape[1]
    piece = proj.shape[2] // QUAD
    ktaps = taps.shape[1]
    groups_here = strip.shape[0]
    group_width = piece // groups_here
    kept = filt.shape[1]
    shard = w.shape[0]
    ncol = w.shape[1] // CHUNKS
    half = length // 2
    rows_step = length // 4
    f32, bf16 = jnp.float32, jnp.bfloat16

    ctx, tp = lax.axis_index("ctx"), lax.axis_index("tp")
    z, r = ctx // QUAD, ctx % QUAD
    lo, c = r // 2, r % 2
    y, hi = tp // 2, tp % 2
    zu, zd = (z + 1) % RING, (z + RING - 1) % RING
    yu, yd = (y + 1) % RING, (y + RING - 1) % RING
    z2, y2 = (z + 2) % RING, (y + 2) % RING

    def flip(s):
        b1 = 1 - lo if s & 2 else lo
        b0 = 1 - c if s & 1 else c
        return 2 * b1 + b0

    def at(ctx_, tp_):
        return {"ctx": ctx_, "tp": tp_}

    up, down = at(zu * QUAD + r, tp), at(zd * QUAD + r, tp)
    right, left = at(ctx, yu * 2 + hi), at(ctx, yd * 2 + hi)
    partner = at(z * QUAD + flip(1), tp)

    def rcopy(src, dst, ssem, rsem, dev):
        return pltpu.make_async_remote_copy(
            src_ref=src, dst_ref=dst, send_sem=ssem, recv_sem=rsem, device_id=dev, device_id_type=MESH
        )

    def landed(dst, rsem):
        pltpu.make_async_copy(dst, dst, rsem).wait()

    sent = []

    def send(src, dst, ssem, rsem, dev):
        copy = rcopy(src, dst, ssem, rsem, dev)
        copy.start()
        sent.append(copy)

    barrier = pltpu.get_barrier_semaphore()
    peers = [at(z * QUAD + flip(s), tp) for s in range(1, QUAD)]
    peers += [at(z * QUAD + s, y * 2 + 1 - hi) for s in range(QUAD)]
    peers += [at(zz * QUAD + s, tp) for zz in (zu, zd) for s in range(QUAD)]
    peers += [right, left]
    for dev in peers:
        pl.semaphore_signal(barrier, inc=1, device_id=dev, device_id_type=MESH)
    pl.semaphore_wait(barrier, len(peers))

    nxt = (ctx + 1) % (QUAD * RING)
    send(proj.at[pl.ds(1, 2), pl.ds(length - RIM, RIM), :], rim, rim_s.at[0], rim_r.at[0], at(nxt, tp))

    fixed = jnp.logical_and(c == hi, hi == lo)
    moves = jnp.logical_not(fixed)
    wdst = at(z * QUAD + 2 * c + hi, y * 2 + lo)

    def wslot(zz, j):
        return wbuf.at[pl.ds(pl.multiple_of(zz * shard, shard), shard), pl.ds(j * ncol, ncol)]

    def wx_copy(j):
        return rcopy(w.at[:, pl.ds(j * ncol, ncol)], wslot(z, j), wx_s.at[j], wx_r.at[j], wdst)

    def wx_start(j):
        @pl.when(fixed)
        def _():
            pltpu.make_async_copy(w.at[:, pl.ds(j * ncol, ncol)], wslot(z, j), wx_r.at[j]).start()

        @pl.when(moves)
        def _():
            wx_copy(j).start()

    def wz_start(j):
        landed(wslot(z, j), wx_r.at[j])
        send(wslot(z, j), wslot(z, j), wz_s.at[j], wz_r.at[j], up)
        send(wslot(z, j), wslot(z, j), wz_s.at[CHUNKS + j], wz_r.at[CHUNKS + j], down)

    def wz_pass(j):
        landed(wslot(zd, j), wz_r.at[j])
        if j in UPWARD:
            send(wslot(zd, j), wslot(zd, j), w2_s.at[j], w2_r.at[j], up)
        landed(wslot(zu, j), wz_r.at[CHUNKS + j])
        if j not in UPWARD:
            send(wslot(zu, j), wslot(zu, j), w2_s.at[j], w2_r.at[j], down)

    wx_start(0)

    tile = half
    ii = lax.broadcasted_iota(jnp.int32, (tile, tile), 0)
    jj = lax.broadcasted_iota(jnp.int32, (tile, tile), 1)
    anti = jnp.where(ii + jj == tile - 1, 1.0, 0.0).astype(bf16)
    for k in range(kept // tile):
        flipped[:, k * tile : (k + 1) * tile] = jnp.dot(
            filt[:, kept - (k + 1) * tile : kept - k * tile], anti, preferred_element_type=f32
        )
    for g in range(groups_here):
        row = flipped[pl.ds(r * groups_here + g, 1), :]
        base = jnp.concatenate([jnp.zeros((1, half), f32), row, jnp.zeros((1, length), f32)], axis=1)
        base = jnp.broadcast_to(base, (16, base.shape[1]))
        base = pltpu.roll(base, 1, 1, stride=1, stride_axis=0)

        def band(k, carry):
            rolled = pltpu.roll(base, 16 * k, 1).astype(bf16)
            start = pl.multiple_of(16 * k, 16)
            strip[g, pl.ds(start, 16), :] = rolled[:, half:]
            strip[g, pl.ds(half + start, 16), :] = rolled[:, : kept + length]
            return carry

        lax.fori_loop(0, half // 16, band, 0)

    def own_rows(rr):
        return pl.ds(pl.multiple_of(kept + rr * length, length), length)

    def halo_rows(rr):
        return pl.ds(pl.multiple_of(rr * length, length), length)

    def mix_piece(s, dst):
        lanes = pl.ds(pl.multiple_of(flip(s) * piece, piece), piece)
        ktap = [taps[1, pl.ds(j, 1), lanes] for j in range(ktaps)]
        vtap = [taps[2, pl.ds(j, 1), lanes] for j in range(ktaps)]

        def rows(i, carry):
            start = pl.multiple_of(i * rows_step - RIM, 16)
            key = proj[1, pl.ds(start, rows_step + RIM), lanes].astype(f32)
            value = proj[2, pl.ds(start, rows_step + RIM), lanes].astype(f32)
            product = short_conv(key, ktap) * short_conv(value, vtap)
            dst[pl.ds(pl.multiple_of(i * rows_step, 16), rows_step), :] = product.astype(bf16)
            return carry

        lax.fori_loop(1, length // rows_step, rows, 0)
        if s == 2:
            landed(rim, rim_r.at[0])
        key = jnp.concatenate([rim[0, :, lanes], proj[1, pl.ds(0, rows_step), lanes]], axis=0).astype(f32)
        value = jnp.concatenate([rim[1, :, lanes], proj[2, pl.ds(0, rows_step), lanes]], axis=0).astype(f32)
        product = short_conv(key, ktap) * short_conv(value, vtap)
        dst[pl.ds(0, rows_step), :] = product.astype(bf16)

    for s in (2, 3, 1):
        mix_piece(s, mixsend.at[s])
        send(mixsend.at[s], seq.at[own_rows(r), :], mix_s.at[s], mix_r.at[s], at(z * QUAD + flip(s), tp))
    mix_piece(0, seq.at[own_rows(r), :])

    def halo_send(s):
        rr = flip(s)
        send(seq.at[own_rows(rr), :], seq.at[halo_rows(rr), :], halo_s.at[s], halo_r.at[rr], up)

    halo_send(0)

    def qrows(rr):
        return pl.ds(pl.multiple_of(RIM + rr * length, 16), length)

    for s in (2, 3, 1):
        lanes = pl.ds(pl.multiple_of(flip(s) * piece, piece), piece)
        send(proj.at[0, :, lanes], qext.at[qrows(r), :], q_s.at[s], q_r.at[s], at(z * QUAD + flip(s), tp))
    mine = pl.ds(pl.multiple_of(r * piece, piece), piece)
    own_query = pltpu.make_async_copy(proj.at[0, :, mine], qext.at[qrows(r), :], q_r.at[0])
    own_query.start()

    def qrim_copy(s):
        return rcopy(
            proj.at[0, pl.ds(length - RIM, RIM), pl.ds(s * piece, piece)],
            qext.at[pl.ds(0, RIM), :],
            qrim_s.at[s], qrim_r.at[0], at(zu * QUAD + s, tp),
        )

    @pl.when(r == QUAD - 1)
    def _():
        for s in range(QUAD):
            qrim_copy(s).start()

    for j in range(1, CHUNKS):
        wx_start(j)

    for s in (1, 2, 3):
        landed(seq.at[own_rows(flip(s)), :], mix_r.at[s])
        halo_send(s)
    wz_start(0)

    landed(qext.at[pl.ds(0, RIM), :], qrim_r.at[0])
    own_query.wait()
    for s in (1, 2, 3):
        landed(qext.at[qrows(flip(s)), :], q_r.at[s])
    qtap = [taps[0, pl.ds(j, 1), mine] for j in range(ktaps)]

    def query_rows(i, carry):
        start = pl.multiple_of(i * rows_step, 16)
        query = qext[pl.ds(start, rows_step + RIM), :].astype(f32)
        qfeat[pl.ds(start, rows_step), :] = short_conv(query, qtap)
        return carry

    lax.fori_loop(0, QUAD * length // rows_step, query_rows, 0)
    wz_start(1)

    gains = gain[:, mine]

    def aslot(yy, cc, b):
        return abuf.at[yy, cc, pl.ds(b * length, length), :]

    for b in ORDER:
        landed(seq.at[pl.ds(b * length, length), :], halo_r.at[b])
        for g in range(groups_here):
            lanes = slice(g * group_width, (g + 1) * group_width)
            window = seq[b * length : b * length + kept + length, lanes]
            toeplitz = jnp.dot(strip[g], window, preferred_element_type=f32)
            skip = gains[:, lanes] * seq[kept + b * length : kept + (b + 1) * length, lanes].astype(f32)
            query = qfeat[b * length : (b + 1) * length, lanes]
            abuf[y, c, b * length : (b + 1) * length, lanes] = (query * (toeplitz + skip)).astype(bf16)
        send(aslot(y, c, b), aslot(y, c, b), a_s.at[b], a_r.at[b], right)
        send(aslot(y, c, b), aslot(y, c, b), a_s.at[4 + b], a_r.at[4 + b], left)
        send(aslot(y, c, b), aslot(y, c, b), a_s.at[8 + b], p_r.at[b], partner)
        if b == 3:
            wz_pass(0)
        if b == 2:
            wz_start(2)

    def a_pass(b):
        landed(aslot(yd, c, b), a_r.at[b])
        if b % 2 == 1:
            send(aslot(yd, c, b), aslot(yd, c, b), a2_s.at[b], a2_r.at[b], right)
        send(aslot(yd, c, b), aslot(yd, c, b), p_s.at[b], p_r.at[4 + b], partner)
        landed(aslot(yu, c, b), a_r.at[4 + b])
        if b % 2 == 0:
            send(aslot(yu, c, b), aslot(yu, c, b), a2_s.at[b], a2_r.at[b], left)
        send(aslot(yu, c, b), aslot(yu, c, b), p_s.at[4 + b], p_r.at[8 + b], partner)

    def a_last(b):
        landed(aslot(y2, c, b), a2_r.at[b])
        send(aslot(y2, c, b), aslot(y2, c, b), p_s.at[8 + b], p_r.at[12 + b], partner)

    a_pass(3)
    wz_pass(1)
    a_pass(2)
    wz_start(3)
    a_pass(1)
    a_pass(0)
    wz_pass(2)
    for b in ORDER:
        a_last(b)
    for b in ORDER:
        for k, yy in enumerate((y, yd, yu, y2)):
            landed(aslot(yy, 1 - c, b), p_r.at[4 * k + b])

    same = c == hi
    apart = jnp.logical_not(same)
    delta = jnp.where(same, 0, 2)

    def c_copy(s, j):
        d = delta + s // 2
        cols = pl.ds(j * ncol, ncol)
        return rcopy(
            csend.at[s, :, cols], crecv.at[d, :, cols], c_s.at[s * CHUNKS + j],
            c_r.at[d * CHUNKS + j], at(z * QUAD + flip(s), y * 2 + c),
        )

    for j in range(CHUNKS):
        landed(wslot(z2, j), w2_r.at[j])
        cols = slice(j * ncol, (j + 1) * ncol)
        for s in (2, 3, 0, 1):
            rows = pl.ds(pl.multiple_of(flip(s) * length, length), length)
            lhs = jnp.concatenate([abuf[k // 2, k % 2, rows, :] for k in range(2 * RING)], axis=1)
            part = jnp.dot(lhs, wbuf[:, cols], preferred_element_type=f32).astype(bf16)
            csend[s, :, cols] = part
            if s == 0:

                @pl.when(same)
                def _():
                    crecv[0, :, cols] = part

                @pl.when(apart)
                def _():
                    c_copy(0, j).start()

            else:
                c_copy(s, j).start()
        if j == 1:
            wz_pass(3)

    for j in range(CHUNKS):
        cols = slice(j * ncol, (j + 1) * ncol)

        @pl.when(apart)
        def _():
            landed(crecv.at[0, :, cols], c_r.at[j])

        for d in range(1, 4):
            landed(crecv.at[d, :, cols], c_r.at[d * CHUNKS + j])
        total = crecv[0, :, cols].astype(f32)
        for d in range(1, 4):
            total = total + crecv[d, :, cols].astype(f32)
        out[:, cols] = total.astype(bf16)

    for copy in sent:
        copy.wait_send()

    @pl.when(moves)
    def _():
        for j in range(CHUNKS):
            wx_copy(j).wait_send()

    @pl.when(r == QUAD - 1)
    def _():
        for s in range(QUAD):
            qrim_copy(s).wait_send()

    @pl.when(apart)
    def _():
        for j in range(CHUNKS):
            c_copy(0, j).wait_send()

    for j in range(CHUNKS):
        for s in range(1, QUAD):
            c_copy(s, j).wait_send()


def local(projected, short_taps, range_filter, skip_gain, out_weight):
    streams, length, width = projected.shape
    piece = width // QUAD
    groups, kept = range_filter.shape
    groups_here = groups // QUAD
    depth, columns = out_weight.shape
    bf16, f32 = jnp.bfloat16, jnp.float32
    vmem = pl.BlockSpec(memory_space=pltpu.VMEM)
    dma = pltpu.SemaphoreType.DMA
    counts = (1, 1, 4, 4, 4, 1, 4, 4, 4, 4, 4, 4, 8, 8, 4, 4, 12, 8, 4, 4, 12, 16, 16, 16)
    return pl.pallas_call(
        kernel,
        out_shape=jax.ShapeDtypeStruct((length, columns), bf16),
        in_specs=[vmem, vmem, vmem, vmem, pl.BlockSpec(memory_space=pl.ANY)],
        out_specs=vmem,
        scratch_shapes=[
            pltpu.VMEM((2, RIM, width), bf16),
            pltpu.VMEM((RIM + QUAD * length, piece), bf16),
            pltpu.VMEM((QUAD * length, piece), f32),
            pltpu.VMEM((QUAD, length, piece), bf16),
            pltpu.VMEM((kept + QUAD * length, piece), bf16),
            pltpu.VMEM((groups, kept), f32),
            pltpu.VMEM((groups_here, length, kept + length), bf16),
            pltpu.VMEM((RING, 2, QUAD * length, piece), bf16),
            pltpu.VMEM((RING * depth, columns), bf16),
            pltpu.VMEM((QUAD, length, columns), bf16),
            pltpu.VMEM((4, length, columns), bf16),
        ]
        + [dma((n,)) for n in counts],
        compiler_params=pltpu.CompilerParams(
            collective_id=0, has_side_effects=True, vmem_limit_bytes=48 * 1024 * 1024
        ),
    )(projected, short_taps, range_filter, skip_gain[None, :], out_weight)


def solution(mesh):
    placed = (P(None, "ctx", "tp"), P(None, None, "tp"), P("tp", None), P("tp"), P("ctx", "tp"))
    return jax.shard_map(
        local, mesh=mesh, in_specs=placed, out_specs=P("ctx", "tp"), check_vma=False
    )
```

time: 259 us -> 82.7 us (0.32)
  waiting for transfers between devices: 166 us -> 0 us
  Pallas kernels: 0 us -> 76.7 us
  local copies, waits for them, and re-layouts: 45.5 us -> 5.72 us
  matrix products: 17.6 us -> 0 us
  between operations: 13.5 us -> 0.01 us
  starting transfers between devices: 9.11 us -> 0 us
  other arithmetic: 7.04 us -> 0 us
    all_gather x2 -> x0, waiting for transfers between devices: 164 us -> none  [the longest x1 92.4 us: local(): lax.all_gather(out_weight, 'ctx', axis=0, tiled=True)]
    pallas_call x0 -> x1, Pallas kernels: none -> 76.7 us  [local(): pl.pallas_call(kernel, out_shape=jax.ShapeDtypeStruct((length, columns),...]
    dot_general x2 -> x0, matrix products: 17.6 us -> none  [the longest x1 12.3 us: local(): jnp.dot(gathered, lax.all_gather(out_weight, 'ctx', axis=0, tiled=True),...]
    reshape x2 -> x0, local copies, waits for them, and re-layouts: 15.4 us -> none  [the longest x1 13.7 us: toeplitz_strip(): tiled[:, start:start + length * (period - 1)]]
    unnamed x11, local copies, waits for them, and re-layouts: 18.2 us -> 5.72 us
    ppermute x5 -> x0, starting transfers between devices: 9.06 us -> none  [passed_along(): return lax.ppermute(block, axis, route)]
    convert_element_type x2 -> x0, other arithmetic: 7.04 us -> none  [the longest x1 5.2 us: local(): mixed_in = (key_feat * value_feat).astype(jnp.bfloat16)]
    slice x4 -> x0, local copies, waits for them, and re-layouts: 7.02 us -> none  [the longest x1 3.92 us: toeplitz_strip(): tiled[:, start:start + length * (period - 1)]]
  transfers between devices with their start and end apart: 7 -> 0, of which waited for: 3 -> 0; matrix products, arithmetic and copies ran while one was open for 15% -> 0% of each run, Pallas kernels for 0% -> 0%
where the time goes in v2:
time: 82.7 us; the launch traced here: 82.4 us
  Pallas kernels  76.7 us (93%)
  local copies, waits for them, and re-layouts  5.72 us (7%)
    pallas_call x1, Pallas kernels, local(): pl.pallas_call(kernel, out_shape=jax.ShapeDtypeStruct((length, columns),...  76.7 us
    unnamed x11, local copies, waits for them, and re-layouts  5.72 us

profile of v2, /device:TPU:1, one launch (start us, length us, event | category | flops | bytes accessed | tf_op | source)
XLA Modules:
  0.0 82.4 jit_solution(6158353151277824841)
XLA Ops:
  0.0 0.0 copy-start
  0.0 1.4 %copy-done = bf16[3,256,1024]{2,1,0:T(8,128)(2,1)S(1)} copy-done((bf16[3,256,1024]{2,1,0:T(8,128)(2,1)S(1)}, bf16[3,256,1024]{2,1,0:T(8,128)(2,1)}, u32[]{:S(2)}) %copy-start) | copy-done | bytes 1572888
  1.4 0.0 copy-start.1
  1.4 1.2 %copy-done.1 = bf16[512,1024]{1,0:T(8,128)(2,1)S(1)} copy-done((bf16[512,1024]{1,0:T(8,128)(2,1)S(1)}, bf16[512,1024]{1,0:T(8,128)(2,1)}, u32[]{:S(2)}) %copy-start.1) | copy-done | bytes 1048600
  2.6 0.0 copy-start.2
  2.6 0.9 %copy-done.2 = f32[3,7,1024]{2,1,0:T(8,128)S(1)} copy-done((f32[3,7,1024]{2,1,0:T(8,128)S(1)}, f32[3,7,1024]{2,1,0:T(8,128)}, u32[]{:S(2)}) %copy-start.2) | copy-done | bytes 86040
  3.5 0.0 copy-start.3
  3.5 0.7 copy-done.3
  4.2 0.0 copy-start.4
  4.2 0.7 copy-done.4
  4.9 76.7 %shard_map.55 = bf16[256,1024]{1,0:T(8,128)(2,1)S(1)} custom-call(bf16[3,256,1024]{2,1,0:T(8,128)(2,1)S(1)} %copy-done, f32[3,7,1024]{2,1,0:T(8,128)S(1)} %copy-done.2, bf16[8,1024]{1,0:T(8,128)(2,1)S(1)} %copy-done.3, f32[1,1024]{1,0:T(1,128)S(1)} %bitcast.1, bf16[512,1024]{1,0:T(8,128)(2,1)S(1)} %copy-done.1), custom_call_target="tpu_custom_call" | custom-call | tf_op jit(solution)/shard_map/pallas_call | solution.py:362
  81.6 0.8 copy.7
Async XLA Ops:
  0.0 1.4 %copy-start = (bf16[3,256,1024]{2,1,0:T(8,128)(2,1)S(1)}, bf16[3,256,1024]{2,1,0:T(8,128)(2,1)}, u32[]{:S(2)}) copy-start(bf16[3,256,1024]{2,1,0:T(8,128)(2,1)} %proj.1) | copy-start | bytes 4718596
  1.4 1.2 %copy-start.1 = (bf16[512,1024]{1,0:T(8,128)(2,1)S(1)}, bf16[512,1024]{1,0:T(8,128)(2,1)}, u32[]{:S(2)}) copy-start(bf16[512,1024]{1,0:T(8,128)(2,1)} %w.1) | copy-start | bytes 3145732
  2.6 0.9 %copy-start.2 = (f32[3,7,1024]{2,1,0:T(8,128)S(1)}, f32[3,7,1024]{2,1,0:T(8,128)}, u32[]{:S(2)}) copy-start(f32[3,7,1024]{2,1,0:T(8,128)} %taps.1) | copy-start | bytes 258052
  3.5 0.7 copy-start.3
  4.2 0.7 copy-start.4

commit v3 on v2

v3 whole, which is shorter than its diff:
```python
import functools

import jax
import jax.numpy as jnp
from jax import lax
from jax.experimental import pallas as pl
from jax.experimental.pallas import tpu as pltpu
from jax.sharding import PartitionSpec as P

MESH = pl.DeviceIdType.MESH
RIM = 16
CUTS = ((0, 4), (4, 4), (8, 4), (12, 2), (14, 2))
CHUNKS = len(CUTS)
RING = 4
QUAD = 4
UPWARD = (2, 4)
ORDER = (3, 1, 2, 0)


def short_conv(extended, tap_rows):
    acc = tap_rows[0] * extended[RIM:]
    for lag in range(1, len(tap_rows)):
        acc = acc + tap_rows[lag] * pltpu.roll(extended, lag, axis=0)[RIM:]
    return acc


def kernel(
    proj, taps_in, filt_in, gain_in, w, out,
    taps, filt, gain, streams, local_s, rim, qext, tsum, mixsend, seq, flipped, strip, abuf, wbuf, csend, crecv,
    rim_s, rim_r, q_s, q_r, qrim_s, qrim_r, mix_s, mix_r, halo_s, halo_r,
    wx_s, wx_r, wz_s, wz_r, w2_s, w2_r, a_s, a_r, a2_s, a2_r, p_s, p_r, c_s, c_r,
):
    length = proj.shape[1]
    piece = proj.shape[2] // QUAD
    ktaps = taps.shape[1]
    groups_here = strip.shape[0]
    group_width = piece // groups_here
    kept = filt.shape[1]
    shard = w.shape[0]
    unit = w.shape[1] // 16
    half = length // 2
    rows_step = length // 4
    f32, bf16 = jnp.float32, jnp.bfloat16

    ctx, tp = lax.axis_index("ctx"), lax.axis_index("tp")
    z, r = ctx // QUAD, ctx % QUAD
    lo, c = r // 2, r % 2
    y, hi = tp // 2, tp % 2
    zu, zd = (z + 1) % RING, (z + RING - 1) % RING
    yu, yd = (y + 1) % RING, (y + RING - 1) % RING
    z2, y2 = (z + 2) % RING, (y + 2) % RING

    def cut(j):
        return pl.ds(CUTS[j][0] * unit, CUTS[j][1] * unit)

    def flip(s):
        b1 = 1 - lo if s & 2 else lo
        b0 = 1 - c if s & 1 else c
        return 2 * b1 + b0

    def at(ctx_, tp_):
        return {"ctx": ctx_, "tp": tp_}

    up, down = at(zu * QUAD + r, tp), at(zd * QUAD + r, tp)
    right, left = at(ctx, yu * 2 + hi), at(ctx, yd * 2 + hi)
    partner = at(z * QUAD + flip(1), tp)

    def rcopy(src, dst, ssem, rsem, dev):
        return pltpu.make_async_remote_copy(
            src_ref=src, dst_ref=dst, send_sem=ssem, recv_sem=rsem, device_id=dev, device_id_type=MESH
        )

    def landed(dst, rsem):
        pltpu.make_async_copy(dst, dst, rsem).wait()

    sent = []

    def send(src, dst, ssem, rsem, dev):
        copy = rcopy(src, dst, ssem, rsem, dev)
        copy.start()
        sent.append(copy)

    barrier = pltpu.get_barrier_semaphore()
    peers = [at(z * QUAD + flip(s), tp) for s in range(1, QUAD)]
    peers += [at(z * QUAD + s, y * 2 + 1 - hi) for s in range(QUAD)]
    peers += [at(zz * QUAD + s, tp) for zz in (zu, zd) for s in range(QUAD)]
    peers += [right, left]
    for dev in peers:
        pl.semaphore_signal(barrier, inc=1, device_id=dev, device_id_type=MESH)
    mine = pl.ds(pl.multiple_of(r * piece, piece), piece)

    def qrows(rr):
        return pl.ds(pl.multiple_of(RIM + rr * length, 16), length)

    loads = [
        pltpu.make_async_copy(src, dst, local_s.at[k])
        for k, (src, dst) in enumerate((
            (taps_in, taps), (proj.at[pl.ds(1, 2)], streams), (filt_in, filt), (gain_in, gain),
            (proj.at[0, :, mine], qext.at[qrows(r), :]),
        ))
    ]
    for load in loads:
        load.start()

    fixed = jnp.logical_and(c == hi, hi == lo)
    moves = jnp.logical_not(fixed)
    wdst = at(z * QUAD + 2 * c + hi, y * 2 + lo)

    def wslot(zz, j):
        return wbuf.at[pl.ds(pl.multiple_of(zz * shard, shard), shard), cut(j)]

    def wx_copy(j):
        return rcopy(w.at[:, cut(j)], wslot(z, j), wx_s.at[j], wx_r.at[j], wdst)

    def wx_start(j):
        @pl.when(fixed)
        def _():
            pltpu.make_async_copy(w.at[:, cut(j)], wslot(z, j), wx_r.at[j]).start()

        @pl.when(moves)
        def _():
            wx_copy(j).start()

    def wz_down(j):
        landed(wslot(z, j), wx_r.at[j])
        send(wslot(z, j), wslot(z, j), wz_s.at[CHUNKS + j], wz_r.at[CHUNKS + j], down)

    def wz_up(j):
        send(wslot(z, j), wslot(z, j), wz_s.at[j], wz_r.at[j], up)

    def from_below(j):
        landed(wslot(zd, j), wz_r.at[j])
        if j in UPWARD:
            send(wslot(zd, j), wslot(zd, j), w2_s.at[j], w2_r.at[j], up)

    def from_above(j):
        landed(wslot(zu, j), wz_r.at[CHUNKS + j])
        if j not in UPWARD:
            send(wslot(zu, j), wslot(zu, j), w2_s.at[j], w2_r.at[j], down)

    def own_rows(rr):
        return pl.ds(pl.multiple_of(kept + rr * length, length), length)

    def halo_rows(rr):
        return pl.ds(pl.multiple_of(rr * length, length), length)

    def mix_dst(s):
        return mixsend.at[s] if s else seq.at[own_rows(r), :]

    def piece_taps(s):
        lanes = pl.ds(pl.multiple_of(flip(s) * piece, piece), piece)
        return lanes, [[taps[m, pl.ds(j, 1), lanes] for j in range(ktaps)] for m in (1, 2)]

    def mix_body(s):
        lanes, (ktap, vtap) = piece_taps(s)
        dst = mix_dst(s)

        def rows(i, carry):
            start = pl.multiple_of(i * rows_step - RIM, 16)
            key = streams[0, pl.ds(start, rows_step + RIM), lanes].astype(f32)
            value = streams[1, pl.ds(start, rows_step + RIM), lanes].astype(f32)
            product = short_conv(key, ktap) * short_conv(value, vtap)
            dst[pl.ds(pl.multiple_of(i * rows_step, 16), rows_step), :] = product.astype(bf16)
            return carry

        lax.fori_loop(1, length // rows_step, rows, 0)

    def mix_head(s):
        lanes, (ktap, vtap) = piece_taps(s)
        key = jnp.concatenate([rim[0, :, lanes], streams[0, pl.ds(0, rows_step), lanes]], axis=0).astype(f32)
        value = jnp.concatenate([rim[1, :, lanes], streams[1, pl.ds(0, rows_step), lanes]], axis=0).astype(f32)
        product = short_conv(key, ktap) * short_conv(value, vtap)
        mix_dst(s)[pl.ds(0, rows_step), :] = product.astype(bf16)

    for load in loads[:2]:
        load.wait()
    for s in (2, 3, 1, 0):
        mix_body(s)

    pl.semaphore_wait(barrier, len(peers))

    nxt = (ctx + 1) % (QUAD * RING)
    send(proj.at[pl.ds(1, 2), pl.ds(length - RIM, RIM), :], rim, rim_s.at[0], rim_r.at[0], at(nxt, tp))

    def qrim_copy(s):
        return rcopy(
            proj.at[0, pl.ds(length - RIM, RIM), pl.ds(s * piece, piece)],
            qext.at[pl.ds(0, RIM), :],
            qrim_s.at[s], qrim_r.at[0], at(zu * QUAD + s, tp),
        )

    @pl.when(r == QUAD - 1)
    def _():
        for s in range(QUAD):
            qrim_copy(s).start()

    parts = (pl.ds(rows_step, length - rows_step), pl.ds(0, rows_step))

    def own_part_rows(rr, part):
        low, size = (rows_step, length - rows_step) if part == 0 else (0, rows_step)
        return pl.ds(pl.multiple_of(kept + rr * length + low, 16), size)

    def halo_part_rows(rr, part):
        low, size = (rows_step, length - rows_step) if part == 0 else (0, rows_step)
        return pl.ds(pl.multiple_of(rr * length + low, 16), size)

    def mix_send(s, part):
        send(
            mixsend.at[s, parts[part], :], seq.at[own_part_rows(r, part), :],
            mix_s.at[2 * s + part], mix_r.at[2 * s + part], at(z * QUAD + flip(s), tp),
        )

    def halo_send(s, part):
        rr = flip(s)
        send(
            seq.at[own_part_rows(rr, part), :], seq.at[halo_part_rows(rr, part), :],
            halo_s.at[2 * s + part], halo_r.at[2 * rr + part], up,
        )

    def mix_pass(s, part):
        landed(seq.at[own_part_rows(flip(s), part), :], mix_r.at[2 * s + part])
        halo_send(s, part)

    wx_start(0)
    for s in (2, 3, 1):
        mix_send(s, 0)
    halo_send(0, 0)

    loads[2].wait()
    tile = half
    ii = lax.broadcasted_iota(jnp.int32, (tile, tile), 0)
    jj = lax.broadcasted_iota(jnp.int32, (tile, tile), 1)
    anti = jnp.where(ii + jj == tile - 1, 1.0, 0.0).astype(bf16)
    ntile = kept // tile
    wide = filt[...].astype(f32)
    stacked = jnp.concatenate([wide[:, k * tile : (k + 1) * tile] for k in range(ntile)], axis=0)
    turned = jnp.dot(stacked.astype(bf16), anti, preferred_element_type=f32)
    rows8 = filt.shape[0]
    for k in range(ntile):
        flipped[:, (ntile - 1 - k) * tile : (ntile - k) * tile] = turned[k * rows8 : (k + 1) * rows8]
    for g in range(groups_here):
        row = flipped[pl.ds(r * groups_here + g, 1), :]
        base = jnp.concatenate([jnp.zeros((1, half), f32), row, jnp.zeros((1, length), f32)], axis=1)
        base = jnp.broadcast_to(base, (16, base.shape[1]))
        base = pltpu.roll(base, 1, 1, stride=1, stride_axis=0)

        def band(k, carry):
            rolled = pltpu.roll(base, 16 * k, 1).astype(bf16)
            start = pl.multiple_of(16 * k, 16)
            strip[g, pl.ds(start, 16), :] = rolled[:, half:]
            strip[g, pl.ds(half + start, 16), :] = rolled[:, : kept + length]
            return carry

        lax.fori_loop(0, half // 16, band, 0)

    landed(rim, rim_r.at[0])
    for s in (2, 3, 1):
        mix_head(s)
        mix_send(s, 1)
    mix_head(0)
    halo_send(0, 1)
    wx_start(1)

    for s in (2, 3, 1):
        lanes = pl.ds(pl.multiple_of(flip(s) * piece, piece), piece)
        send(proj.at[0, :, lanes], qext.at[qrows(r), :], q_s.at[s], q_r.at[s], at(z * QUAD + flip(s), tp))
    for j in range(2, CHUNKS):
        wx_start(j)

    mix_pass(1, 0)
    mix_pass(1, 1)
    mix_pass(2, 0)
    mix_pass(3, 0)
    wz_down(0)
    for s in (2, 3):
        mix_pass(s, 1)
    wz_up(0)

    loads[3].wait()
    gains = gain[:, mine]
    for b in range(QUAD - 1, -1, -1):
        for part in (0, 1):
            landed(seq.at[halo_part_rows(b, part), :], halo_r.at[2 * b + part])
        for g in range(groups_here):
            lanes = slice(g * group_width, (g + 1) * group_width)
            window = seq[b * length : b * length + kept + length, lanes]
            toeplitz = jnp.dot(strip[g], window, preferred_element_type=f32)
            skip = gains[:, lanes] * seq[kept + b * length : kept + (b + 1) * length, lanes].astype(f32)
            tsum[b * length : (b + 1) * length, lanes] = toeplitz + skip

    wz_down(1)
    wz_up(1)

    landed(qext.at[pl.ds(0, RIM), :], qrim_r.at[0])
    loads[4].wait()
    for s in (1, 2, 3):
        landed(qext.at[qrows(flip(s)), :], q_r.at[s])
    qtap = [taps[0, pl.ds(j, 1), mine] for j in range(ktaps)]

    def aslot(yy, cc, b):
        return abuf.at[yy, cc, pl.ds(b * length, length), :]

    def gate(b):
        def gate_rows(i, carry):
            start = pl.multiple_of(b * length + i * rows_step, 16)
            query = short_conv(qext[pl.ds(start, rows_step + RIM), :].astype(f32), qtap)
            abuf[y, c, pl.ds(start, rows_step), :] = (query * tsum[pl.ds(start, rows_step), :]).astype(bf16)
            return carry

        lax.fori_loop(0, length // rows_step, gate_rows, 0)

    def a_send(b):
        gate(b)
        send(aslot(y, c, b), aslot(y, c, b), a_s.at[b], a_r.at[b], right)
        send(aslot(y, c, b), aslot(y, c, b), a_s.at[4 + b], a_r.at[4 + b], left)
        send(aslot(y, c, b), aslot(y, c, b), a_s.at[8 + b], p_r.at[b], partner)

    def a_pass(b):
        landed(aslot(yd, c, b), a_r.at[b])
        if b >= 2:
            send(aslot(yd, c, b), aslot(yd, c, b), a2_s.at[b], a2_r.at[b], right)
        send(aslot(yd, c, b), aslot(yd, c, b), p_s.at[b], p_r.at[4 + b], partner)
        landed(aslot(yu, c, b), a_r.at[4 + b])
        if b < 2:
            send(aslot(yu, c, b), aslot(yu, c, b), a2_s.at[b], a2_r.at[b], left)
        send(aslot(yu, c, b), aslot(yu, c, b), p_s.at[4 + b], p_r.at[8 + b], partner)

    def a_last(b):
        landed(aslot(y2, c, b), a2_r.at[b])
        send(aslot(y2, c, b), aslot(y2, c, b), p_s.at[8 + b], p_r.at[12 + b], partner)

    same = c == hi
    apart = jnp.logical_not(same)
    delta = jnp.where(same, 0, 2)

    def c_copy(b, j):
        d = delta + (1 - lo if b >= 2 else lo)
        cols = cut(j)
        return rcopy(
            csend.at[b, :, cols], crecv.at[d, :, cols], c_s.at[b * CHUNKS + j],
            c_r.at[d * CHUNKS + j], at(z * QUAD + b, y * 2 + c),
        )

    def own_part(b):
        return jnp.logical_and(same, r == b)

    def c_step(b, j):
        cols = cut(j)
        lhs = jnp.concatenate(
            [abuf[k // 2, k % 2, b * length : (b + 1) * length, :] for k in range(2 * RING)], axis=1
        )
        part = jnp.dot(lhs, wbuf[:, cols], preferred_element_type=f32).astype(bf16)
        csend[b, :, cols] = part

        @pl.when(own_part(b))
        def _():
            crecv[0, :, cols] = part

        @pl.when(jnp.logical_not(own_part(b)))
        def _():
            c_copy(b, j).start()

    def a_other(b):
        for k, yy in enumerate((y, yd, yu, y2)):
            landed(aslot(yy, 1 - c, b), p_r.at[4 * k + b])

    def finish(j):
        cols = cut(j)

        @pl.when(apart)
        def _():
            landed(crecv.at[0, :, cols], c_r.at[j])

        for d in range(1, 4):
            landed(crecv.at[d, :, cols], c_r.at[d * CHUNKS + j])
        total = crecv[0, :, cols].astype(f32)
        for d in range(1, 4):
            total = total + crecv[d, :, cols].astype(f32)
        out[:, cols] = total.astype(bf16)

    first, second, third, fourth = ORDER

    def w_ready(j):
        landed(wslot(z2, j), w2_r.at[j])

    a_send(first)
    a_send(second)
    from_above(0)
    a_pass(first)
    a_send(third)
    from_above(1)
    wz_down(2)
    wz_up(2)
    a_pass(second)
    a_send(fourth)
    for j in (3, 4):
        wz_down(j)
        wz_up(j)
    a_last(first)
    from_below(0)
    w_ready(0)
    a_other(first)
    c_step(first, 0)
    a_pass(third)
    a_last(second)
    a_pass(fourth)
    from_below(2)
    a_other(second)
    c_step(second, 0)
    from_below(1)
    w_ready(1)
    c_step(first, 1)
    c_step(second, 1)
    a_last(third)
    a_last(fourth)
    from_below(4)
    a_other(third)
    c_step(third, 0)
    c_step(third, 1)
    a_other(fourth)
    c_step(fourth, 0)
    c_step(fourth, 1)
    from_above(3)
    from_above(2)
    w_ready(2)
    for b in ORDER:
        c_step(b, 2)
    from_above(4)
    w_ready(4)
    for b in ORDER:
        c_step(b, 4)
    from_below(3)
    w_ready(3)
    for b in ORDER:
        c_step(b, 3)
    finish(0)
    for j in range(1, CHUNKS):
        finish(j)

    for copy in sent:
        copy.wait_send()

    @pl.when(moves)
    def _():
        for j in range(CHUNKS):
            wx_copy(j).wait_send()

    @pl.when(r == QUAD - 1)
    def _():
        for s in range(QUAD):
            qrim_copy(s).wait_send()

    for b in range(QUAD):

        @pl.when(jnp.logical_not(own_part(b)))
        def _():
            for j in range(CHUNKS):
                c_copy(b, j).wait_send()


def local(projected, short_taps, range_filter, skip_gain, out_weight):
    streams, length, width = projected.shape
    piece = width // QUAD
    groups, kept = range_filter.shape
    groups_here = groups // QUAD
    depth, columns = out_weight.shape
    bf16, f32 = jnp.bfloat16, jnp.float32
    hbm = pl.BlockSpec(memory_space=pltpu.HBM)
    dma = pltpu.SemaphoreType.DMA
    nc = CHUNKS
    counts = (1, 1, 4, 4, 4, 1, 8, 8, 8, 8, nc, nc, 2 * nc, 2 * nc, nc, nc, 12, 8, 4, 4, 12, 16, 4 * nc, 4 * nc)
    return pl.pallas_call(
        kernel,
        out_shape=jax.ShapeDtypeStruct((length, columns), bf16),
        in_specs=[hbm] * 5,
        out_specs=pl.BlockSpec(memory_space=pltpu.VMEM),
        scratch_shapes=[
            pltpu.VMEM(short_taps.shape, f32),
            pltpu.VMEM((groups, kept), bf16),
            pltpu.VMEM((1, width), f32),
            pltpu.VMEM((2, length, width), bf16),
            dma((5,)),
            pltpu.VMEM((2, RIM, width), bf16),
            pltpu.VMEM((RIM + QUAD * length, piece), bf16),
            pltpu.VMEM((QUAD * length, piece), f32),
            pltpu.VMEM((QUAD, length, piece), bf16),
            pltpu.VMEM((kept + QUAD * length, piece), bf16),
            pltpu.VMEM((groups, kept), f32),
            pltpu.VMEM((groups_here, length, kept + length), bf16),
            pltpu.VMEM((RING, 2, QUAD * length, piece), bf16),
            pltpu.VMEM((RING * depth, columns), bf16),
            pltpu.VMEM((QUAD, length, columns), bf16),
            pltpu.VMEM((4, length, columns), bf16),
        ]
        + [dma((n,)) for n in counts],
        compiler_params=pltpu.CompilerParams(
            collective_id=0, has_side_effects=True, vmem_limit_bytes=50 * 1024 * 1024
        ),
    )(*[pltpu.with_memory_space_constraint(v, pltpu.HBM) for v in (projected, short_taps, range_filter, skip_gain[None, :], out_weight)])


def solution(mesh):
    placed = (P(None, "ctx", "tp"), P(None, None, "tp"), P("tp", None), P("tp"), P("ctx", "tp"))
    return jax.shard_map(
        local, mesh=mesh, in_specs=placed, out_specs=P("ctx", "tp"), check_vma=False
    )
```

time: 82.7 us -> 74.3 us (0.90)
  local copies, waits for them, and re-layouts: 5.72 us -> 0.8 us
  Pallas kernels: 76.7 us -> 73.3 us
    unnamed x11 -> x1, local copies, waits for them, and re-layouts: 5.72 us -> 0.8 us
    pallas_call x1, Pallas kernels: 76.7 us -> 73.3 us  [local(): pl.pallas_call(kernel, out_shape=jax.ShapeDtypeStruct((length, columns),...]
where the time goes in v3:
time: 74.3 us; the launch traced here: 74.1 us
  Pallas kernels  73.3 us (99%)
  local copies, waits for them, and re-layouts  0.8 us (1%)
    pallas_call x1, Pallas kernels, local(): pl.pallas_call(kernel, out_shape=jax.ShapeDtypeStruct((length, columns),...  73.3 us

profile of v3, /device:TPU:1, one launch (start us, length us, event | category | flops | bytes accessed | tf_op | source)
XLA Modules:
  0.0 74.1 jit_solution(599226169611294322)
XLA Ops:
  0.0 73.3 %shard_map.55 = bf16[256,1024]{1,0:T(8,128)(2,1)S(1)} custom-call(bf16[3,256,1024]{2,1,0:T(8,128)(2,1)} %proj.1, f32[3,7,1024]{2,1,0:T(8,128)} %taps_in.1, bf16[8,1024]{1,0:T(8,128)(2,1)} %filt_in.1, f32[1,1024]{1,0:T(1,128)} %bitcast.1, bf16[512,1024]{1,0:T(8,128)(2,1)} %w.1), custom_call_target="tpu_custom_call" | custom-call | tf_op jit(solution)/shard_map/pallas_call | solution.py:472
  73.3 0.8 %copy.7 = bf16[256,1024]{1,0:T(8,128)(2,1)} copy(bf16[256,1024]{1,0:T(8,128)(2,1)S(1)} %shard_map.55) | data formatting | bytes 1048576

commit v4 on v3

--- a/solution.py
+++ b/solution.py
@@ -11,9 +11,10 @@
 RIM = 16
 CUTS = ((0, 4), (4, 4), (8, 4), (12, 2), (14, 2))
 CHUNKS = len(CUTS)
+TO_RIM, TO_QRIM, TO_MIX, TO_HALO, TO_X, TO_Z, TO_A, TO_C = range(8)
 RING = 4
 QUAD = 4
-UPWARD = (2, 4)
+UPWARD = (2, 3, 4)
 ORDER = (3, 1, 2, 0)
 
 
@@ -27,8 +28,7 @@
 def kernel(
     proj, taps_in, filt_in, gain_in, w, out,
     taps, filt, gain, streams, local_s, rim, qext, tsum, mixsend, seq, flipped, strip, abuf, wbuf, csend, crecv,
-    rim_s, rim_r, q_s, q_r, qrim_s, qrim_r, mix_s, mix_r, halo_s, halo_r,
-    wx_s, wx_r, wz_s, wz_r, w2_s, w2_r, a_s, a_r, a2_s, a2_r, p_s, p_r, c_s, c_r,
+    sends, rim_r, q_r, qrim_r, mix_r, halo_r, wx_r, wz_r, w2_r, a_r, a2_r, p_r, c_r,
 ):
     length = proj.shape[1]
     piece = proj.shape[2] // QUAD
@@ -73,12 +73,8 @@
     def landed(dst, rsem):
         pltpu.make_async_copy(dst, dst, rsem).wait()
 
-    sent = []
-
-    def send(src, dst, ssem, rsem, dev):
-        copy = rcopy(src, dst, ssem, rsem, dev)
-        copy.start()
-        sent.append(copy)
+    def send(src, dst, kind, rsem, dev):
+        rcopy(src, dst, sends.at[kind], rsem, dev).start()
 
     barrier = pltpu.get_barrier_semaphore()
     peers = [at(z * QUAD + flip(s), tp) for s in range(1, QUAD)]
@@ -93,7 +89,7 @@
         return pl.ds(pl.multiple_of(RIM + rr * length, 16), length)
 
     loads = [
-        pltpu.make_async_copy(src, dst, local_s.at[k])
+        pltpu.make_async_copy(src, dst, q_r.at[0] if k == 4 else local_s.at[k])
         for k, (src, dst) in enumerate((
             (taps_in, taps), (proj.at[pl.ds(1, 2)], streams), (filt_in, filt), (gain_in, gain),
             (proj.at[0, :, mine], qext.at[qrows(r), :]),
@@ -107,36 +103,50 @@
     wdst = at(z * QUAD + 2 * c + hi, y * 2 + lo)
 
     def wslot(zz, j):
-        return wbuf.at[pl.ds(pl.multiple_of(zz * shard, shard), shard), cut(j)]
+        return wbuf[j].at[pl.ds(pl.multiple_of(zz * shard, shard), shard), :]
 
     def wx_copy(j):
-        return rcopy(w.at[:, cut(j)], wslot(z, j), wx_s.at[j], wx_r.at[j], wdst)
+        return rcopy(w.at[:, cut(j)], wslot(z, j), sends.at[TO_X], wx_r.at[j], wdst)
 
     def wx_start(j):
-        @pl.when(fixed)
-        def _():
-            pltpu.make_async_copy(w.at[:, cut(j)], wslot(z, j), wx_r.at[j]).start()
-
         @pl.when(moves)
         def _():
             wx_copy(j).start()
 
+    def z_copy(j, src, upward):
+        if upward:
+            return rcopy(src, wslot(z, j), sends.at[TO_Z], wz_r.at[j], up)
+        return rcopy(src, wslot(z, j), sends.at[TO_Z], wz_r.at[CHUNKS + j], down)
+
+    def fixed_start(upward):
+        @pl.when(fixed)
+        def _():
+            for j in range(CHUNKS):
+                if not upward:
+                    pltpu.make_async_copy(w.at[:, cut(j)], wslot(z, j), wx_r.at[j]).start()
+                z_copy(j, w.at[:, cut(j)], upward).start()
+
     def wz_down(j):
         landed(wslot(z, j), wx_r.at[j])
-        send(wslot(z, j), wslot(z, j), wz_s.at[CHUNKS + j], wz_r.at[CHUNKS + j], down)
+
+        @pl.when(moves)
+        def _():
+            z_copy(j, wslot(z, j), False).start()
 
     def wz_up(j):
-        send(wslot(z, j), wslot(z, j), wz_s.at[j], wz_r.at[j], up)
+        @pl.when(moves)
+        def _():
+            z_copy(j, wslot(z, j), True).start()
 
     def from_below(j):
         landed(wslot(zd, j), wz_r.at[j])
         if j in UPWARD:
-            send(wslot(zd, j), wslot(zd, j), w2_s.at[j], w2_r.at[j], up)
+            send(wslot(zd, j), wslot(zd, j), TO_Z, w2_r.at[j], up)
 
     def from_above(j):
         landed(wslot(zu, j), wz_r.at[CHUNKS + j])
         if j not in UPWARD:
-            send(wslot(zu, j), wslot(zu, j), w2_s.at[j], w2_r.at[j], down)
+            send(wslot(zu, j), wslot(zu, j), TO_Z, w2_r.at[j], down)
 
     def own_rows(rr):
         return pl.ds(pl.multiple_of(kept + rr * length, length), length)
@@ -180,13 +190,13 @@
     pl.semaphore_wait(barrier, len(peers))
 
     nxt = (ctx + 1) % (QUAD * RING)
-    send(proj.at[pl.ds(1, 2), pl.ds(length - RIM, RIM), :], rim, rim_s.at[0], rim_r.at[0], at(nxt, tp))
+    send(proj.at[pl.ds(1, 2), pl.ds(length - RIM, RIM), :], rim, TO_RIM, rim_r.at[0], at(nxt, tp))
 
     def qrim_copy(s):
         return rcopy(
             proj.at[0, pl.ds(length - RIM, RIM), pl.ds(s * piece, piece)],
             qext.at[pl.ds(0, RIM), :],
-            qrim_s.at[s], qrim_r.at[0], at(zu * QUAD + s, tp),
+            sends.at[TO_QRIM], qrim_r.at[0], at(zu * QUAD + s, tp),
         )
 
     @pl.when(r == QUAD - 1)
@@ -207,21 +217,20 @@
     def mix_send(s, part):
         send(
             mixsend.at[s, parts[part], :], seq.at[own_part_rows(r, part), :],
-            mix_s.at[2 * s + part], mix_r.at[2 * s + part], at(z * QUAD + flip(s), tp),
+            TO_MIX, mix_r.at[2 * s + part], at(z * QUAD + flip(s), tp),
         )
 
     def halo_send(s, part):
         rr = flip(s)
         send(
             seq.at[own_part_rows(rr, part), :], seq.at[halo_part_rows(rr, part), :],
-            halo_s.at[2 * s + part], halo_r.at[2 * rr + part], up,
+            TO_HALO, halo_r.at[rr], up,
         )
 
     def mix_pass(s, part):
         landed(seq.at[own_part_rows(flip(s), part), :], mix_r.at[2 * s + part])
         halo_send(s, part)
 
-    wx_start(0)
     for s in (2, 3, 1):
         mix_send(s, 0)
     halo_send(0, 0)
@@ -259,28 +268,29 @@
         mix_send(s, 1)
     mix_head(0)
     halo_send(0, 1)
-    wx_start(1)
-
-    for s in (2, 3, 1):
-        lanes = pl.ds(pl.multiple_of(flip(s) * piece, piece), piece)
-        send(proj.at[0, :, lanes], qext.at[qrows(r), :], q_s.at[s], q_r.at[s], at(z * QUAD + flip(s), tp))
-    for j in range(2, CHUNKS):
-        wx_start(j)
+    wx_start(0)
+    fixed_start(False)
 
     mix_pass(1, 0)
     mix_pass(1, 1)
     mix_pass(2, 0)
     mix_pass(3, 0)
-    wz_down(0)
     for s in (2, 3):
         mix_pass(s, 1)
+
+    for s in (2, 3, 1):
+        lanes = pl.ds(pl.multiple_of(flip(s) * piece, piece), piece)
+        send(proj.at[0, :, lanes], qext.at[qrows(r), :], TO_MIX, q_r.at[0], at(z * QUAD + flip(s), tp))
+    for j in range(1, CHUNKS):
+        wx_start(j)
+    fixed_start(True)
+    wz_down(0)
     wz_up(0)
 
     loads[3].wait()
     gains = gain[:, mine]
     for b in range(QUAD - 1, -1, -1):
-        for part in (0, 1):
-            landed(seq.at[halo_part_rows(b, part), :], halo_r.at[2 * b + part])
+        landed(seq.at[pl.ds(b * length, length), :], halo_r.at[b])
         for g in range(groups_here):
             lanes = slice(g * group_width, (g + 1) * group_width)
             window = seq[b * length : b * length + kept + length, lanes]
@@ -288,95 +298,93 @@
             skip = gains[:, lanes] * seq[kept + b * length : kept + (b + 1) * length, lanes].astype(f32)
             tsum[b * length : (b + 1) * length, lanes] = toeplitz + skip
 
-    wz_down(1)
-    wz_up(1)
-
     landed(qext.at[pl.ds(0, RIM), :], qrim_r.at[0])
-    loads[4].wait()
-    for s in (1, 2, 3):
-        landed(qext.at[qrows(flip(s)), :], q_r.at[s])
+    landed(qext.at[pl.ds(RIM, QUAD * length), :], q_r.at[0])
     qtap = [taps[0, pl.ds(j, 1), mine] for j in range(ktaps)]
 
     def aslot(yy, cc, b):
-        return abuf.at[yy, cc, pl.ds(b * length, length), :]
+        return abuf.at[2 * yy + cc, pl.ds(b * length, length), :]
+
+    def slots(count):
+        return abuf.at[pl.ds(0, count)]
 
     def gate(b):
         def gate_rows(i, carry):
             start = pl.multiple_of(b * length + i * rows_step, 16)
             query = short_conv(qext[pl.ds(start, rows_step + RIM), :].astype(f32), qtap)
-            abuf[y, c, pl.ds(start, rows_step), :] = (query * tsum[pl.ds(start, rows_step), :]).astype(bf16)
+            abuf[2 * y + c, pl.ds(start, rows_step), :] = (query * tsum[pl.ds(start, rows_step), :]).astype(bf16)
             return carry
 
         lax.fori_loop(0, length // rows_step, gate_rows, 0)
 
     def a_send(b):
         gate(b)
-        send(aslot(y, c, b), aslot(y, c, b), a_s.at[b], a_r.at[b], right)
-        send(aslot(y, c, b), aslot(y, c, b), a_s.at[4 + b], a_r.at[4 + b], left)
-        send(aslot(y, c, b), aslot(y, c, b), a_s.at[8 + b], p_r.at[b], partner)
+        send(aslot(y, c, b), aslot(y, c, b), TO_A, a_r.at[b], right)
+        send(aslot(y, c, b), aslot(y, c, b), TO_A, a_r.at[4 + b], left)
+        send(aslot(y, c, b), aslot(y, c, b), TO_A, p_r.at[b], partner)
 
     def a_pass(b):
         landed(aslot(yd, c, b), a_r.at[b])
         if b >= 2:
-            send(aslot(yd, c, b), aslot(yd, c, b), a2_s.at[b], a2_r.at[b], right)
-        send(aslot(yd, c, b), aslot(yd, c, b), p_s.at[b], p_r.at[4 + b], partner)
+            send(aslot(yd, c, b), aslot(yd, c, b), TO_A, a2_r.at[b], right)
+        send(aslot(yd, c, b), aslot(yd, c, b), TO_A, p_r.at[b], partner)
         landed(aslot(yu, c, b), a_r.at[4 + b])
         if b < 2:
-            send(aslot(yu, c, b), aslot(yu, c, b), a2_s.at[b], a2_r.at[b], left)
-        send(aslot(yu, c, b), aslot(yu, c, b), p_s.at[4 + b], p_r.at[8 + b], partner)
+            send(aslot(yu, c, b), aslot(yu, c, b), TO_A, a2_r.at[b], left)
+        send(aslot(yu, c, b), aslot(yu, c, b), TO_A, p_r.at[b], partner)
 
     def a_last(b):
         landed(aslot(y2, c, b), a2_r.at[b])
-        send(aslot(y2, c, b), aslot(y2, c, b), p_s.at[8 + b], p_r.at[12 + b], partner)
+        send(aslot(y2, c, b), aslot(y2, c, b), TO_A, p_r.at[b], partner)
 
     same = c == hi
     apart = jnp.logical_not(same)
     delta = jnp.where(same, 0, 2)
 
-    def c_copy(b, j):
+    def c_copy(b, g):
         d = delta + (1 - lo if b >= 2 else lo)
-        cols = cut(j)
+        rsem = c_r.at[jnp.where(d == 0, CHUNKS, 0) + g]
         return rcopy(
-            csend.at[b, :, cols], crecv.at[d, :, cols], c_s.at[b * CHUNKS + j],
-            c_r.at[d * CHUNKS + j], at(z * QUAD + b, y * 2 + c),
+            csend[g].at[b], crecv[g].at[d], sends.at[TO_C],
+            rsem, at(z * QUAD + b, y * 2 + c),
         )
 
     def own_part(b):
         return jnp.logical_and(same, r == b)
 
-    def c_step(b, j):
-        cols = cut(j)
+    def c_step(b, first_group, count=1):
         lhs = jnp.concatenate(
-            [abuf[k // 2, k % 2, b * length : (b + 1) * length, :] for k in range(2 * RING)], axis=1
+            [abuf[k, b * length : (b + 1) * length, :] for k in range(2 * RING)], axis=1
         )
-        part = jnp.dot(lhs, wbuf[:, cols], preferred_element_type=f32).astype(bf16)
-        csend[b, :, cols] = part
-
-        @pl.when(own_part(b))
-        def _():
-            crecv[0, :, cols] = part
-
-        @pl.when(jnp.logical_not(own_part(b)))
-        def _():
-            c_copy(b, j).start()
+        groups = range(first_group, first_group + count)
+        rhs = wbuf[first_group][...] if count == 1 else jnp.concatenate([wbuf[g][...] for g in groups], axis=1)
+        part = jnp.dot(lhs, rhs, preferred_element_type=f32).astype(bf16)
+        low = CUTS[first_group][0]
+        for g in groups:
+            here = part[:, (CUTS[g][0] - low) * unit : (sum(CUTS[g]) - low) * unit]
+            csend[g][b] = here
+
+            @pl.when(own_part(b))
+            def _():
+                crecv[g][0] = here
+
+            @pl.when(jnp.logical_not(own_part(b)))
+            def _():
+                c_copy(b, g).start()
 
     def a_other(b):
-        for k, yy in enumerate((y, yd, yu, y2)):
-            landed(aslot(yy, 1 - c, b), p_r.at[4 * k + b])
-
-    def finish(j):
-        cols = cut(j)
-
+        landed(slots(1), p_r.at[b])
+
+    def finish(g):
         @pl.when(apart)
         def _():
-            landed(crecv.at[0, :, cols], c_r.at[j])
-
+            landed(crecv[g].at[0], c_r.at[CHUNKS + g])
+
+        landed(crecv[g].at[pl.ds(1, 3)], c_r.at[g])
+        total = crecv[g][0].astype(f32)
         for d in range(1, 4):
-            landed(crecv.at[d, :, cols], c_r.at[d * CHUNKS + j])
-        total = crecv[0, :, cols].astype(f32)
-        for d in range(1, 4):
-            total = total + crecv[d, :, cols].astype(f32)
-        out[:, cols] = total.astype(bf16)
+            total = total + crecv[g][d].astype(f32)
+        out[:, cut(g)] = total.astype(bf16)
 
     first, second, third, fourth = ORDER
 
@@ -385,6 +393,8 @@
 
     a_send(first)
     a_send(second)
+    wz_down(1)
+    wz_up(1)
     from_above(0)
     a_pass(first)
     a_send(third)
@@ -413,49 +423,43 @@
     c_step(second, 1)
     a_last(third)
     a_last(fourth)
+    from_below(3)
     from_below(4)
     a_other(third)
-    c_step(third, 0)
-    c_step(third, 1)
+    c_step(third, 0, 2)
     a_other(fourth)
-    c_step(fourth, 0)
-    c_step(fourth, 1)
-    from_above(3)
-    from_above(2)
-    w_ready(2)
-    for b in ORDER:
-        c_step(b, 2)
-    from_above(4)
-    w_ready(4)
-    for b in ORDER:
-        c_step(b, 4)
-    from_below(3)
-    w_ready(3)
-    for b in ORDER:
-        c_step(b, 3)
-    finish(0)
-    for j in range(1, CHUNKS):
-        finish(j)
-
-    for copy in sent:
-        copy.wait_send()
+    c_step(fourth, 0, 2)
+    for j in range(2, CHUNKS):
+        from_above(j)
+        if j not in UPWARD:
+            from_below(j)
+        w_ready(j)
+        for b in ORDER:
+            c_step(b, j)
+    for g in range(CHUNKS):
+        finish(g)
+
+    landed(rim, sends.at[TO_RIM])
+    landed(seq.at[pl.ds(0, 6 * length), :], sends.at[TO_MIX])
+    landed(seq.at[pl.ds(0, 4 * length), :], sends.at[TO_HALO])
+    landed(slots(6), sends.at[TO_Z])
+    landed(slots(7), sends.at[TO_A])
 
     @pl.when(moves)
     def _():
-        for j in range(CHUNKS):
-            wx_copy(j).wait_send()
+        landed(slots(2), sends.at[TO_X])
 
     @pl.when(r == QUAD - 1)
     def _():
-        for s in range(QUAD):
-            qrim_copy(s).wait_send()
-
-    for b in range(QUAD):
-
-        @pl.when(jnp.logical_not(own_part(b)))
-        def _():
-            for j in range(CHUNKS):
-                c_copy(b, j).wait_send()
+        landed(seq.at[pl.ds(0, QUAD * RIM), :], sends.at[TO_QRIM])
+
+    @pl.when(same)
+    def _():
+        landed(slots(3), sends.at[TO_C])
+
+    @pl.when(apart)
+    def _():
+        landed(slots(4), sends.at[TO_C])
 
 
 def local(projected, short_taps, range_filter, skip_gain, out_weight):
@@ -468,7 +472,8 @@
     hbm = pl.BlockSpec(memory_space=pltpu.HBM)
     dma = pltpu.SemaphoreType.DMA
     nc = CHUNKS
-    counts = (1, 1, 4, 4, 4, 1, 8, 8, 8, 8, nc, nc, 2 * nc, 2 * nc, nc, nc, 12, 8, 4, 4, 12, 16, 4 * nc, 4 * nc)
+    widths = [size * columns // 16 for _, size in CUTS]
+    counts = (8, 1, 1, 1, 8, 4, nc, 2 * nc, nc, 8, 4, 4, 2 * nc)
     return pl.pallas_call(
         kernel,
         out_shape=jax.ShapeDtypeStruct((length, columns), bf16),
@@ -487,10 +492,10 @@
             pltpu.VMEM((kept + QUAD * length, piece), bf16),
             pltpu.VMEM((groups, kept), f32),
             pltpu.VMEM((groups_here, length, kept + length), bf16),
-            pltpu.VMEM((RING, 2, QUAD * length, piece), bf16),
-            pltpu.VMEM((RING * depth, columns), bf16),
-            pltpu.VMEM((QUAD, length, columns), bf16),
-            pltpu.VMEM((4, length, columns), bf16),
+            pltpu.VMEM((RING * 2, QUAD * length, piece), bf16),
+            tuple(pltpu.VMEM((RING * depth, wide), bf16) for wide in widths),
+            tuple(pltpu.VMEM((QUAD, length, wide), bf16) for wide in widths),
+            tuple(pltpu.VMEM((4, length, wide), bf16) for wide in widths),
         ]
         + [dma((n,)) for n in counts],
         compiler_params=pltpu.CompilerParams(

time: 74.3 us -> 69.4 us (0.934)
  Pallas kernels: 73.3 us -> 68 us
    pallas_call x1, Pallas kernels: 73.3 us -> 68 us  [local(): pl.pallas_call(kernel, out_shape=jax.ShapeDtypeStruct((length, columns),...]
where the time goes in v4:
time: 69.4 us; the launch traced here: 68.8 us
  Pallas kernels  68 us (98%)
  local copies, waits for them, and re-layouts  0.8 us (1%)
    pallas_call x1, Pallas kernels, local(): pl.pallas_call(kernel, out_shape=jax.ShapeDtypeStruct((length, columns),...  68 us

profile of v4, /device:TPU:1, one launch (start us, length us, event | category | flops | bytes accessed | tf_op | source)
XLA Modules:
  0.0 68.8 jit_solution(14912882970594907714)
XLA Ops:
  0.0 68.0 %shard_map.55 = bf16[256,1024]{1,0:T(8,128)(2,1)S(1)} custom-call(bf16[3,256,1024]{2,1,0:T(8,128)(2,1)} %proj.1, f32[3,7,1024]{2,1,0:T(8,128)} %taps_in.1, bf16[8,1024]{1,0:T(8,128)(2,1)} %filt_in.1, f32[1,1024]{1,0:T(1,128)} %bitcast.1, bf16[512,1024]{1,0:T(8,128)(2,1)} %w.1), custom_call_target="tpu_custom_call" | custom-call | tf_op jit(solution)/shard_map/pallas_call | solution.py:477
  68.0 0.8 %copy.7 = bf16[256,1024]{1,0:T(8,128)(2,1)} copy(bf16[256,1024]{1,0:T(8,128)(2,1)S(1)} %shard_map.55) | data formatting | bytes 1048576

commit v5 on v4

--- a/solution.py
+++ b/solution.py
@@ -15,6 +15,7 @@
 RING = 4
 QUAD = 4
 UPWARD = (2, 3, 4)
+EARLY = (0, 1)
 ORDER = (3, 1, 2, 0)
 
 
@@ -108,8 +109,11 @@
     def wx_copy(j):
         return rcopy(w.at[:, cut(j)], wslot(z, j), sends.at[TO_X], wx_r.at[j], wdst)
 
+    soon = jnp.logical_and(lo != hi, c == hi)
+    soon_here = jnp.logical_and(lo != hi, c == lo)
+
     def wx_start(j):
-        @pl.when(moves)
+        @pl.when(jnp.logical_and(moves, jnp.logical_not(soon)))
         def _():
             wx_copy(j).start()
 
@@ -127,9 +131,13 @@
                 z_copy(j, w.at[:, cut(j)], upward).start()
 
     def wz_down(j):
-        landed(wslot(z, j), wx_r.at[j])
-
-        @pl.when(moves)
+        late = jnp.logical_not(soon_here) if j in EARLY else True
+
+        @pl.when(late)
+        def _():
+            landed(wslot(z, j), wx_r.at[j])
+
+        @pl.when(jnp.logical_and(moves, late))
         def _():
             z_copy(j, wslot(z, j), False).start()
 
@@ -230,6 +238,11 @@
     def mix_pass(s, part):
         landed(seq.at[own_part_rows(flip(s), part), :], mix_r.at[2 * s + part])
         halo_send(s, part)
+
+    @pl.when(soon)
+    def _():
+        for j in range(CHUNKS):
+            wx_copy(j).start()
 
     for s in (2, 3, 1):
         mix_send(s, 0)
@@ -277,6 +290,12 @@
     mix_pass(3, 0)
     for s in (2, 3):
         mix_pass(s, 1)
+
+    @pl.when(soon_here)
+    def _():
+        for j in EARLY:
+            landed(wslot(z, j), wx_r.at[j])
+            z_copy(j, wslot(z, j), False).start()
 
     for s in (2, 3, 1):
         lanes = pl.ds(pl.multiple_of(flip(s) * piece, piece), piece)

time: 69.4 us -> 69.4 us (level)
  no operation moved by 1% of the time
where the time goes in v5:
time: 69.4 us; the launch traced here: 69.3 us
  Pallas kernels  68.5 us (99%)
  local copies, waits for them, and re-layouts  0.8 us (1%)
    pallas_call x1, Pallas kernels, local(): pl.pallas_call(kernel, out_shape=jax.ShapeDtypeStruct((length, columns),...  68.5 us

profile of v5, /device:TPU:1, one launch (start us, length us, event | category | flops | bytes accessed | tf_op | source)
XLA Modules:
  0.0 69.3 jit_solution(8422880330933482086)
XLA Ops:
  0.0 68.5 %shard_map.55 = bf16[256,1024]{1,0:T(8,128)(2,1)S(1)} custom-call(bf16[3,256,1024]{2,1,0:T(8,128)(2,1)} %proj.1, f32[3,7,1024]{2,1,0:T(8,128)} %taps_in.1, bf16[8,1024]{1,0:T(8,128)(2,1)} %filt_in.1, f32[1,1024]{1,0:T(1,128)} %bitcast.1, bf16[512,1024]{1,0:T(8,128)(2,1)} %w.1), custom_call_target="tpu_custom_call" | custom-call | tf_op jit(solution)/shard_map/pallas_call | solution.py:496
  68.5 0.8 %copy.7 = bf16[256,1024]{1,0:T(8,128)(2,1)} copy(bf16[256,1024]{1,0:T(8,128)(2,1)S(1)} %shard_map.55) | data formatting | bytes 1048576

commit v6 on v5

--- a/solution.py
+++ b/solution.py
@@ -90,13 +90,18 @@
         return pl.ds(pl.multiple_of(RIM + rr * length, 16), length)
 
     loads = [
-        pltpu.make_async_copy(src, dst, q_r.at[0] if k == 4 else local_s.at[k])
+        pltpu.make_async_copy(src, dst, q_r.at[0] if k == 3 else local_s.at[k])
         for k, (src, dst) in enumerate((
-            (taps_in, taps), (proj.at[pl.ds(1, 2)], streams), (filt_in, filt), (gain_in, gain),
+            (taps_in, taps), (filt_in, filt), (gain_in, gain),
             (proj.at[0, :, mine], qext.at[qrows(r), :]),
         ))
     ]
-    for load in loads:
+    lanes_of = [pl.ds(pl.multiple_of(flip(s) * piece, piece), piece) for s in (2, 3, 1, 0)]
+    piece_loads = [
+        pltpu.make_async_copy(proj.at[pl.ds(1, 2), :, lanes], streams.at[:, :, lanes], local_s.at[3 + k])
+        for k, lanes in enumerate(lanes_of)
+    ]
+    for load in loads[:1] + piece_loads + loads[1:]:
         load.start()
 
     fixed = jnp.logical_and(c == hi, hi == lo)
@@ -190,9 +195,9 @@
         product = short_conv(key, ktap) * short_conv(value, vtap)
         mix_dst(s)[pl.ds(0, rows_step), :] = product.astype(bf16)
 
-    for load in loads[:2]:
-        load.wait()
-    for s in (2, 3, 1, 0):
+    loads[0].wait()
+    for k, s in enumerate((2, 3)):
+        piece_loads[k].wait()
         mix_body(s)
 
     pl.semaphore_wait(barrier, len(peers))
@@ -244,11 +249,16 @@
         for j in range(CHUNKS):
             wx_copy(j).start()
 
-    for s in (2, 3, 1):
+    for s in (2, 3):
         mix_send(s, 0)
+    piece_loads[2].wait()
+    mix_body(1)
+    mix_send(1, 0)
+    piece_loads[3].wait()
+    mix_body(0)
     halo_send(0, 0)
 
-    loads[2].wait()
+    loads[1].wait()
     tile = half
     ii = lax.broadcasted_iota(jnp.int32, (tile, tile), 0)
     jj = lax.broadcasted_iota(jnp.int32, (tile, tile), 1)
@@ -288,9 +298,6 @@
     mix_pass(1, 1)
     mix_pass(2, 0)
     mix_pass(3, 0)
-    for s in (2, 3):
-        mix_pass(s, 1)
-
     @pl.when(soon_here)
     def _():
         for j in EARLY:
@@ -302,20 +309,32 @@
         send(proj.at[0, :, lanes], qext.at[qrows(r), :], TO_MIX, q_r.at[0], at(z * QUAD + flip(s), tp))
     for j in range(1, CHUNKS):
         wx_start(j)
+    for s in (2, 3):
+        mix_pass(s, 1)
+
+
+    loads[2].wait()
+    gains = gain[:, mine]
+    def window_dot(b, g, first_block, last_block):
+        lanes = slice(g * group_width, (g + 1) * group_width)
+        rows = slice((b + first_block) * length, (b + last_block) * length)
+        return jnp.dot(
+            strip[g, :, first_block * length : last_block * length], seq[rows, lanes], preferred_element_type=f32
+        )
+
+    for b in range(QUAD - 1, -1, -1):
+        for g in range(groups_here):
+            lanes = slice(g * group_width, (g + 1) * group_width)
+            skip = gains[:, lanes] * seq[kept + b * length : kept + (b + 1) * length, lanes].astype(f32)
+            tsum[b * length : (b + 1) * length, lanes] = skip + window_dot(b, g, QUAD - b, QUAD + 1)
     fixed_start(True)
     wz_down(0)
     wz_up(0)
-
-    loads[3].wait()
-    gains = gain[:, mine]
     for b in range(QUAD - 1, -1, -1):
         landed(seq.at[pl.ds(b * length, length), :], halo_r.at[b])
         for g in range(groups_here):
             lanes = slice(g * group_width, (g + 1) * group_width)
-            window = seq[b * length : b * length + kept + length, lanes]
-            toeplitz = jnp.dot(strip[g], window, preferred_element_type=f32)
-            skip = gains[:, lanes] * seq[kept + b * length : kept + (b + 1) * length, lanes].astype(f32)
-            tsum[b * length : (b + 1) * length, lanes] = toeplitz + skip
+            tsum[b * length : (b + 1) * length, lanes] += window_dot(b, g, 0, QUAD - b)
 
     landed(qext.at[pl.ds(0, RIM), :], qrim_r.at[0])
     landed(qext.at[pl.ds(RIM, QUAD * length), :], q_r.at[0])
@@ -503,7 +522,7 @@
             pltpu.VMEM((groups, kept), bf16),
             pltpu.VMEM((1, width), f32),
             pltpu.VMEM((2, length, width), bf16),
-            dma((5,)),
+            dma((7,)),
             pltpu.VMEM((2, RIM, width), bf16),
             pltpu.VMEM((RIM + QUAD * length, piece), bf16),
             pltpu.VMEM((QUAD * length, piece), f32),

time: 69.4 us -> 69 us (level)
  no operation moved by 1% of the time
where the time goes in v6:
time: 69 us; the launch traced here: 68.9 us
  Pallas kernels  68.1 us (99%)
  local copies, waits for them, and re-layouts  0.8 us (1%)
    pallas_call x1, Pallas kernels, local(): pl.pallas_call(kernel, out_shape=jax.ShapeDtypeStruct((length, columns),...  68.1 us

profile of v6, /device:TPU:1, one launch (start us, length us, event | category | flops | bytes accessed | tf_op | source)
XLA Modules:
  0.0 68.9 jit_solution(6343513122270354934)
XLA Ops:
  0.0 68.1 %shard_map.55 = bf16[256,1024]{1,0:T(8,128)(2,1)S(1)} custom-call(bf16[3,256,1024]{2,1,0:T(8,128)(2,1)} %proj.1, f32[3,7,1024]{2,1,0:T(8,128)} %taps_in.1, bf16[8,1024]{1,0:T(8,128)(2,1)} %filt_in.1, f32[1,1024]{1,0:T(1,128)} %bitcast.1, bf16[512,1024]{1,0:T(8,128)(2,1)} %w.1), custom_call_target="tpu_custom_call" | custom-call | tf_op jit(solution)/shard_map/pallas_call | solution.py:515
  68.1 0.8 %copy.7 = bf16[256,1024]{1,0:T(8,128)(2,1)} copy(bf16[256,1024]{1,0:T(8,128)(2,1)S(1)} %shard_map.55) | data formatting | bytes 1048576

commit v7 on v6

--- a/solution.py
+++ b/solution.py
@@ -16,7 +16,7 @@
 QUAD = 4
 UPWARD = (2, 3, 4)
 EARLY = (0, 1)
-ORDER = (3, 1, 2, 0)
+ORDER = (0, 2, 1, 3)
 
 
 def short_conv(extended, tap_rows):

time: 69 us -> 68.7 us (level)
  no operation moved by 1% of the time
where the time goes in v7:
time: 68.7 us; the launch traced here: 68.6 us
  Pallas kernels  67.8 us (99%)
  local copies, waits for them, and re-layouts  0.8 us (1%)
    pallas_call x1, Pallas kernels, local(): pl.pallas_call(kernel, out_shape=jax.ShapeDtypeStruct((length, columns),...  67.8 us

profile of v7, /device:TPU:1, one launch (start us, length us, event | category | flops | bytes accessed | tf_op | source)
XLA Modules:
  0.0 68.6 jit_solution(14256173120072536810)
XLA Ops:
  0.0 67.8 %shard_map.55 = bf16[256,1024]{1,0:T(8,128)(2,1)S(1)} custom-call(bf16[3,256,1024]{2,1,0:T(8,128)(2,1)} %proj.1, f32[3,7,1024]{2,1,0:T(8,128)} %taps_in.1, bf16[8,1024]{1,0:T(8,128)(2,1)} %filt_in.1, f32[1,1024]{1,0:T(1,128)} %bitcast.1, bf16[512,1024]{1,0:T(8,128)(2,1)} %w.1), custom_call_target="tpu_custom_call" | custom-call | tf_op jit(solution)/shard_map/pallas_call | solution.py:515
  67.8 0.8 %copy.7 = bf16[256,1024]{1,0:T(8,128)(2,1)} copy(bf16[256,1024]{1,0:T(8,128)(2,1)S(1)} %shard_map.55) | data formatting | bytes 1048576
